TPU v7x, 128 devices: a whole 4x4x4 slice. The times are simulated.
128 devices in a mesh: seq: 32 (over z_hi, y, x), head: 4 (over z_lo, core).
Axes of the slice: x: 4, y: 4, z: 4 (z_hi: 2, z_lo: 2; z = z_hi * 2 + z_lo), core: 2. Of those that a mesh axis runs over, the one named last changes fastest.
Arguments:
- x_in: bfloat16 [16384, 4096], P('seq', 'head'), may hold values from -6 to 6
- z_in: bfloat16 [16384, 4096], P('seq', 'head'), may hold values from -6 to 6
- b_in: bfloat16 [16384, 512], P('seq', 'head'), may hold values from -0.5 to 0.5
- c_in: bfloat16 [16384, 512], P('seq', 'head'), may hold values from -0.5 to 0.5
- dt_raw: float32 [64, 16384], P('head', 'seq')
- dt_bias: float32 [64], P('head'), may hold values from -5 to -4
- a_log: float32 [64], P('head')
- d_skip: float32 [64], P('head'), may hold values from 0.1 to 1.9
- gain: float32 [4096], P('head'), may hold values from 0.5 to 1.5
- resets: int32 [64, 128], P('head', 'seq'), may hold values 0 or 1
- out_weight: bfloat16 [4096, 4096], P('seq', 'head'), may hold values from -0.09375 to 0.09375
- cotangent: bfloat16 [16384, 4096], P('seq', 'head'), may hold values from -6 to 6
Outputs:
- d_x: bfloat16 [16384, 4096], P('seq', 'head')
- d_z: bfloat16 [16384, 4096], P('seq', 'head')
- d_b: bfloat16 [16384, 512], P('seq', 'head')
- d_c: bfloat16 [16384, 512], P('seq', 'head')
- raw_timestep_gradient: float32 [64, 16384], P('head', 'seq')
- d_out_weight: float32 [4096, 4096], P('seq', 'head')
All inputs are finite; a program needn't handle non-finite values. No bound on the sum of `resets` on one device may be relied on, other than what follows from the above.
Results may differ from a plain program's by a relative error of at most 0.0075.
Values may be sent and summed in bfloat16 or wider, within the bound.
A program may use at most 256 MiB of HBM per device.

v0:
```python
from functools import partial

import jax
import jax.numpy as jnp
from jax import lax
from jax.sharding import PartitionSpec as P

HEADDIM = 64
STATE = 128
BLOCK = 128


highest = lax.Precision.HIGHEST


def prefix(value, axis, join, neutral, backward):
    count, mine = (lax.axis_size(axis), lax.axis_index(axis))
    pieces = jax.tree.map(lambda part: lax.all_gather(part, axis), value)
    if backward:
        pieces = jax.tree.map(lambda part: part[::-1], pieces)
        mine = count - 1 - mine
    so_far = jax.tree.map(
        lambda part, zero: jnp.full_like(part, 0) + jnp.asarray(zero, part.dtype), value, neutral
    )

    def step(position, so_far):
        longer = join(so_far, jax.tree.map(lambda part: part[position], pieces))
        return jax.tree.map(lambda new, old: jnp.where(position < mine, new, old), longer, so_far)

    return lax.fori_loop(0, count - 1, step, so_far)


def block_step(state, inputs, per_group, skip_gain):
    x_block, b_block, c_block, rate_block, step_block, keep_block = inputs
    running = jnp.cumsum(rate_block, axis=1)
    positions = rate_block.shape[1]
    lower = jnp.arange(positions)[:, None] >= jnp.arange(positions)[None, :]
    spread = jnp.where(lower[None], running[:, :, None] - running[:, None, :], 0.0)
    decays = jnp.exp(spread) * lower[None].astype(jnp.float32)
    scores = jnp.einsum("tgn,sgn->gts", c_block, b_block, precision=highest)
    scores = jnp.repeat(scores, per_group, axis=0)
    mixing = scores * decays * step_block[:, None, :]
    within = jnp.einsum("hts,shp->thp", mixing, x_block, precision=highest)
    c_heads = jnp.repeat(c_block, per_group, axis=1)
    b_heads = jnp.repeat(b_block, per_group, axis=1)
    carried = state * keep_block[:, None, None]
    incoming = (
        jnp.einsum("thn,hpn->thp", c_heads, carried, precision=highest)
        * jnp.exp(running).T[:, :, None]
    )
    output = within + incoming + skip_gain[None, :, None] * x_block
    weighted = (jnp.exp(running[:, -1:] - running) * step_block).T
    fresh = jnp.einsum("sh,shp,shn->hpn", weighted, x_block, b_heads, precision=highest)
    return (carried * jnp.exp(running[:, -1])[:, None, None] + fresh, output)


def scan_blocks(inputs, bmatrix, cmatrix, dt_raw, start, dt_bias, a_log, d_skip, keep):
    positions = inputs.shape[0]
    heads = dt_raw.shape[0]
    groups = bmatrix.shape[1] // STATE
    blocks = positions // BLOCK
    step_size = jax.nn.softplus(dt_raw + dt_bias[:, None])
    rate = -step_size * jnp.exp(a_log)[:, None]
    x_blocks = inputs.reshape(blocks, BLOCK, heads, HEADDIM)
    b_blocks = bmatrix.reshape(blocks, BLOCK, groups, STATE)
    c_blocks = cmatrix.reshape(blocks, BLOCK, groups, STATE)
    rate_blocks = rate.reshape(heads, blocks, BLOCK).transpose(1, 0, 2)
    step_blocks = step_size.reshape(heads, blocks, BLOCK).transpose(1, 0, 2)
    stepper = partial(block_step, per_group=heads // groups, skip_gain=d_skip)
    final, outputs = lax.scan(
        stepper, start, (x_blocks, b_blocks, c_blocks, rate_blocks, step_blocks, keep.T)
    )
    return (outputs.reshape(positions, heads * HEADDIM), final)


def gate_norm(mixed, gates, gain, groups):
    gated = mixed * jax.nn.silu(gates)
    count = gated.shape[0]
    grouped = gated.reshape(count, groups, -1)
    factor = lax.rsqrt(jnp.mean(grouped * grouped, axis=2, keepdims=True) + 1e-05)
    return (grouped * factor).reshape(count, -1) * gain


def compose(earlier, later):
    return (earlier[0] * later[0], later[0][:, None, None] * earlier[1] + later[1])


def body(
    x_in, z_in, b_in, c_in, dt_raw, dt_bias, a_log, d_skip, gain, resets, out_weight, cotangent
):
    heads = dt_raw.shape[0]
    groups = b_in.shape[1] // STATE
    per_group = heads // groups
    positions = x_in.shape[0]
    keep = 1.0 - resets.astype(jnp.float32)
    x_wide = x_in.astype(jnp.float32)
    input_matrix_wide = b_in.astype(jnp.float32)
    c_wide = c_in.astype(jnp.float32)
    z_wide = z_in.astype(jnp.float32)
    zero_state = jnp.zeros((heads, HEADDIM, STATE), jnp.float32)
    step_size = jax.nn.softplus(dt_raw + dt_bias[:, None])
    rate = -step_size * jnp.exp(a_log)[:, None]
    running = jnp.cumsum(rate, axis=1)
    suffix_rates = jnp.flip(jnp.cumsum(jnp.flip(rate, axis=1), axis=1), axis=1)
    after_rates = jnp.concatenate([suffix_rates[:, 1:], jnp.zeros((heads, 1), jnp.float32)], axis=1)
    keep_upto = jnp.repeat(jnp.cumprod(keep, axis=1), BLOCK, axis=1)
    keep_suffix = jnp.flip(jnp.cumprod(jnp.flip(keep, axis=1), axis=1), axis=1)
    keep_after = jnp.concatenate([keep_suffix[:, 1:], jnp.ones((heads, 1), jnp.float32)], axis=1)
    keep_after = jnp.repeat(keep_after, BLOCK, axis=1)
    to_end = jnp.exp(after_rates) * keep_after * step_size
    x_heads = x_wide.reshape(positions, groups, per_group, HEADDIM)
    b_groups = input_matrix_wide.reshape(positions, groups, STATE)
    c_groups = c_wide.reshape(positions, groups, STATE)
    end_weights = to_end.T.reshape(positions, groups, per_group)
    local_final = jnp.einsum(
        "tgq,tgqp,tgn->gqpn", end_weights, x_heads, b_groups, precision=highest
    ).reshape(heads, HEADDIM, STATE)
    slab_decay = jnp.exp(running[:, -1]) * jnp.prod(keep, axis=1)
    identity = (jnp.ones((heads,), jnp.float32), zero_state)
    entering = prefix((slab_decay, local_final), "seq", compose, identity, False)[1]

    def mixer(x_value, b_value, c_value, raw_steps, start_state):
        return scan_blocks(
            x_value, b_value, c_value, raw_steps, start_state, dt_bias, a_log, d_skip, keep
        )

    (mixed, leaving), mixer_pull = jax.vjp(
        mixer, x_wide, input_matrix_wide, c_wide, dt_raw, entering
    )

    def norming(mixed_value, z_value):
        return gate_norm(mixed_value, z_value, gain, groups)

    normed, norm_pull = jax.vjp(norming, mixed, z_wide)
    normed_half = normed.astype(jnp.bfloat16)
    gathered = lax.all_gather(cotangent, "head", axis=1, tiled=True)
    columns = gathered
    d_normed = jnp.dot(
        columns,
        lax.all_gather(out_weight, "seq", axis=0, tiled=True),
        preferred_element_type=jnp.float32,
    )
    d_mixed, grad_z = norm_pull(d_normed)
    from_start = (jnp.exp(running) * keep_upto).T.reshape(positions, groups, per_group)
    d_heads = d_mixed.reshape(positions, groups, per_group, HEADDIM)
    start_grad = jnp.einsum(
        "tgq,tgqp,tgn->gqpn", from_start, d_heads, c_groups, precision=highest
    ).reshape(heads, HEADDIM, STATE)
    arriving = prefix((slab_decay, start_grad), "seq", compose, identity, True)[1]
    grad_x, grad_b, grad_c, grad_steps, unused = mixer_pull((d_mixed, arriving))
    columns = gathered
    d_out_weight = lax.psum_scatter(
        jnp.einsum("td,ti->di", columns, normed_half, preferred_element_type=jnp.float32),
        "seq",
        scatter_dimension=0,
        tiled=True,
    )
    return (
        grad_x.astype(jnp.bfloat16),
        grad_z.astype(jnp.bfloat16),
        grad_b.astype(jnp.bfloat16),
        grad_c.astype(jnp.bfloat16),
        grad_steps,
        d_out_weight,
    )


def solution(mesh):
    return jax.shard_map(
        body,
        mesh=mesh,
        in_specs=(
            P("seq", "head"),
            P("seq", "head"),
            P("seq", "head"),
            P("seq", "head"),
            P("head", "seq"),
            P("head"),
            P("head"),
            P("head"),
            P("head"),
            P("head", "seq"),
            P("seq", "head"),
            P("seq", "head"),
        ),
        out_specs=(
            P("seq", "head"),
            P("seq", "head"),
            P("seq", "head"),
            P("seq", "head"),
            P("head", "seq"),
            P("seq", "head"),
        ),
        check_vma=False,
    )
```

profile of v0, /device:TPU:0, one launch (start us, length us, event | category | flops | bytes accessed | tf_op | source)
XLA Modules:
  0.0 738.4 jit_solution(9167421800133413308)
XLA Ops:
  14.2 1.9 fusion.107
  21.2 96.0 %all-gather.2 = f32[32,1,16]{2,1,0:T(1,128)S(1)} all-gather(f32[1,1,16]{2,1,0:T(1,128)S(1)} %fusion.127), channel_id=1, replica_groups=mesh['seq'=32,'head'=4] {'seq'}, dimensions={0}, use_global_device_ids=true | all-gather | bytes 2112 | tf_op jit(solution)/shard_map/all_gather | solution.py:18
  117.3 1.9 copy.146
  120.9 54.4 %all-gather.12.cloned.1.call-done = f32[512,64,128]{2,1,0:T(8,128)} async-done(((f32[16,64,128]{2,1,0:T(8,128)}), f32[512,64,128]{2,1,0:T(8,128)}) %all-gather.12.cloned.1.call-update) | async-done | bytes 16777232 | tf_op jit(solution)/shard_map/all_gather | solution.py:18
  175.3 37.9 %while.110 = (s32[]{:T(128)}, f32[16,64,128]{2,1,0:T(8,128)S(1)}, s32[]{:T(128)}, f32[32,16]{1,0:T(8,128)S(1)}, f32[32,16,64,128]{3,2,1,0:T(8,128)}) while((s32[]{:T(128)}, f32[16,64,128]{2,1,0:T(8,128)S(1)}, s32[]{:T(128)}, f32[32,16]{1,0:T(8,128)S(1)}, f32[32,16,64,128]{3,2,1,0:T(8,128)}) %tuple.254), condition=%wide.region_8.9_spmd.clone.clone, body=%wide.region_7.8_spmd.clone.sunk.clone | while | flops 524292 | bytes 1573145 | solution.py:30
  216.0 83.1 %while.109 = (s32[]{:T(128)}, f32[16,64,128]{2,1,0:T(8,128)S(1)}, f32[4,128,16,64]{1,3,2,0:T(8,128)}, f32[4,16,128,128]{3,2,1,0:T(8,128)}, f32[4,16,128,128]{3,2...) while((s32[]{:T(128)}, f32[16,64,128]{2,1,0:T(8,128)S(1)}, ...), condition=%wide.region_11.12_spmd.clone.clone.clone, body=%wide.region_9.11_spmd.clone.clone.sunk.clone | while | flops 633511936 | bytes 16000793 | solution.py:70
  219.2 2.9 multiply_dynamic-update-slice_fusion.3
  222.1 3.0 bitcast_dynamic-update-slice_fusion.23
  225.1 3.7 fusion.254
  239.9 2.9 multiply_dynamic-update-slice_fusion.3
  242.9 3.0 bitcast_dynamic-update-slice_fusion.23
  245.9 3.7 fusion.254
  260.7 2.9 multiply_dynamic-update-slice_fusion.3
  263.7 2.9 bitcast_dynamic-update-slice_fusion.23
  266.6 3.7 fusion.254
  281.3 3.2 multiply_dynamic-update-slice_fusion.3
  284.5 3.0 bitcast_dynamic-update-slice_fusion.23
  287.5 3.7 fusion.254
  299.2 4.7 copy.179
  303.9 4.8 reshape.531
  308.8 21.7 %all-gather.10.cloned.1.call-done = bf16[4096,1024]{1,0:T(8,128)(2,1)} async-done(((bf16[128,1024]{1,0:T(8,128)(2,1)}), bf16[4096,1024]{1,0:T(8,128)(2,1)}) %all-gather.10.cloned.1.call-update) | async-done | bytes 8388624 | tf_op jit(solution)/shard_map/all_gather | solution.py:140
  330.4 10.6 %multiply_reduce_fusion.1 = (f32[512]{0:T(512)S(1)}, f32[512]{0:T(512)S(1)}, f32[512,1024]{1,0:T(8,128)S(1)}) fusion(f32[512,1024]{1,0:T(8,128)} %reshape.531, bf16[512,1024]{1,0:T(8,128)(2,1)} %param.21, f32[1024]{0:T(1024)S(1)} %copy-done.15, bf16[512,4096]{1,0:T(8,128)(2,1)} %all-gather.8.cloned.1.call-done, ...), kind=kOutput, calls=%fused_computation.184 | convolution fusion | flops 4300733440 | bytes 17833984 | tf_op jit(solution)/shard_map/dot_general | solution.py:138
  341.0 3.6 fusion.104
  344.6 2.0 copy.149
  346.6 3.5 fusion.105
  350.1 13.9 %convolution_bitcast_fusion.4 = f32[4096,1024]{0,1:T(8,128)} fusion(bf16[512,4096]{1,0:T(8,128)(2,1)} %all-gather.8.cloned.1.call-done, f32[512]{0:T(512)S(1)} %get-tuple-element.1859, f32[1024]{0:T(1024)S(1)} %copy-done.15, f32[512,1024]{1,0:T(8,128)} %reshape.531, bf16[512,1024]{1,0:T(8,128)(2,1)} %param.21), kind=kOutput, calls=%fused_computation.168 | convolution fusion | flops 4299685888 | bytes 24123392 | tf_op jit(solution)/shard_map/td,ti->di/dot_general | solution.py:153
  366.1 2.6 reshape.529
  368.8 3.1 copy.152
  371.8 132.6 %all-gather.14.cloned.1.call-done = f32[512,64,128]{2,1,0:T(8,128)} async-done(((f32[16,64,128]{2,1,0:T(8,128)}), f32[512,64,128]{2,1,0:T(8,128)}) %all-gather.14.cloned.1.call-update) | async-done | bytes 16777232 | tf_op jit(solution)/shard_map/all_gather | solution.py:18
  504.5 11.8 %rev.19 = f32[32,16,64,128]{3,2,1,0:T(8,128)} reverse(f32[32,16,64,128]{3,2,1,0:T(8,128)} %bitcast.594), dimensions={0} | reverse | bytes 33554432 | tf_op jit(solution)/shard_map/rev | solution.py:20
  516.3 37.7 %while.111 = (s32[]{:T(128)}, f32[16,64,128]{2,1,0:T(8,128)S(1)}, s32[]{:T(128)}, f32[32,16]{1,0:T(8,128)S(1)}, f32[32,16,64,128]{3,2,1,0:T(8,128)}) while((s32[]{:T(128)}, f32[16,64,128]{2,1,0:T(8,128)S(1)}, s32[]{:T(128)}, f32[32,16]{1,0:T(8,128)S(1)}, f32[32,16,64,128]{3,2,1,0:T(8,128)}) %tuple.234), condition=%wide.region_15.16_spmd.clone.clone, body=%wide.region_14.15_spmd.clone.sunk.clone | while | flops 524292 | bytes 1573145 | solution.py:30
  556.7 163.1 %while.108 = (s32[]{:T(128)}, f32[16,64,128]{2,1,0:T(8,128)S(1)}, bf16[4,128,16,64]{1,3,2,0:T(8,128)(2,1)}, bf16[4,128,1,128]{3,1,2,0:T(8,128)(2,1)}, bf16[4,128...) while((s32[]{:T(128)}, f32[16,64,128]{2,1,0:T(8,128)S(1)}, ...), condition=%wide.region_25.26_spmd.clone.clone, body=%wide.region_16.25_spmd.clone.sunk.clone | while | flops 1263466496 | bytes 32037560 | solution.py:70
  556.9 2.7 constant_dynamic-slice_fusion.16
  559.6 3.3 fusion.236
  564.5 2.1 fusion.243
  567.2 5.0 fusion.238
  585.5 3.1 fusion.237
  588.6 2.0 convolution_bitcast_fusion.9
  593.5 2.1 convolution_bitcast_fusion.10
  597.7 2.7 constant_dynamic-slice_fusion.16
  600.3 3.3 fusion.236
  605.2 2.1 fusion.243
  608.0 5.0 fusion.238
  626.3 3.1 fusion.237
  629.4 2.0 convolution_bitcast_fusion.9
  634.2 2.1 convolution_bitcast_fusion.10
  638.3 2.7 constant_dynamic-slice_fusion.16
  641.0 3.3 fusion.236
  645.9 2.1 fusion.243
  648.7 5.0 fusion.238
  666.9 3.1 fusion.237
  670.0 2.0 convolution_bitcast_fusion.9
  674.8 2.1 convolution_bitcast_fusion.10
  679.0 2.7 constant_dynamic-slice_fusion.16
  681.7 3.3 fusion.236
  686.6 2.1 fusion.243
  689.3 5.0 fusion.238
  707.6 3.1 fusion.237
  710.7 2.0 convolution_bitcast_fusion.9
  715.6 2.1 convolution_bitcast_fusion.10
  720.8 2.7 copy.177
  723.5 2.3 reshape.530
  726.6 3.0 reduce-scatter.2.cloned.1.call-done
  729.6 2.0 copy.166
  (455 shorter events, 223.0 us)
Async XLA Ops:
  7.2 168.2 %all-gather.12.cloned.1.call-start = ((), (), s32[]{:S(2)}) async-start(), calls=%async_computation.4 | async-start | bytes 17301504 | tf_op jit(solution)/shard_map/all_gather | solution.py:18
  7.9 0.9 copy-start.16
  13.3 0.8 copy-start.5
  13.3 0.8 copy-start.13
  13.3 0.9 copy-start.3
  14.2 3.5 copy-start.12
  16.2 292.6 %all-gather.8.cloned.1.call-start = ((), (), s32[]{:S(2)}) async-start(), calls=%async_computation.1 | async-start | bytes 5242880 | tf_op jit(solution)/shard_map/all_gather | solution.py:136
  16.9 313.5 %all-gather.10.cloned.1.call-start = ((), (), s32[]{:S(2)}) async-start(), calls=%async_computation.2 | async-start | bytes 8650752 | tf_op jit(solution)/shard_map/all_gather | solution.py:140
  17.6 486.8 %all-gather.14.cloned.1.call-start = ((), (), s32[]{:S(2)}) async-start(), calls=%async_computation.5 | async-start | bytes 17301504 | tf_op jit(solution)/shard_map/all_gather | solution.py:18
  117.3 1.9 copy-start.4
  299.2 4.8 copy-start.1
  303.9 26.5 %copy-start.15 = (f32[1024]{0:T(1024)S(1)}, f32[1024]{0:T(1024)}, u32[]{:S(2)}) copy-start(f32[1024]{0:T(1024)} %param.28) | copy-start | bytes 12292
  330.4 10.6 %copy-start.2 = (f32[512,1024]{1,0:T(8,128)S(1)}, f32[512,1024]{1,0:T(8,128)}, u32[]{:S(2)}) copy-start(f32[512,1024]{1,0:T(8,128)} %reshape.531) | copy-start | bytes 6291460
  350.1 379.5 %reduce-scatter.2.cloned.1.call-start = ((), (), s32[]{:S(2)}) async-start(), calls=%async_computation.3 | async-start | bytes 17301504 | tf_op jit(solution)/shard_map/reduce_scatter | solution.py:152
  585.5 6.6 copy-start
  590.6 5.8 copy-start.9
  592.1 4.6 copy-start.7
  596.7 0.7 copy-start.10
  597.0 0.7 copy-start.8
  626.3 6.5 copy-start
  631.4 5.7 copy-start.9
  632.7 4.6 copy-start.7
  637.3 0.7 copy-start.10
  637.7 0.7 copy-start.8
  666.9 6.5 copy-start
  672.0 5.8 copy-start.9
  673.4 4.6 copy-start.7
  678.0 0.7 copy-start.10
  678.4 0.7 copy-start.8
  707.6 6.6 copy-start
  712.8 5.8 copy-start.9
  714.2 4.6 copy-start.7
  718.8 0.7 copy-start.10
  719.1 0.7 copy-start.8
  723.5 2.3 copy-start.6
  723.5 2.3 copy-start.11
  723.5 2.3 copy-start.14
  723.5 2.3 copy-start.17
Sparse Core Ops, SparseCore 0:
  16.3 159.0 all-gather.11
  177.0 43.7 all-gather.7
  223.9 106.4 all-gather.9
  350.2 154.2 all-gather.13
  506.7 222.8 reduce-scatter.1
where the time goes:
time: 749 us; the launch traced here: 738 us
  waiting for transfers between devices  213 us (28%)
  other arithmetic  151 us (20%)
  local copies, waits for them, and re-layouts  131 us (17%)
  matrix products  131 us (17%)
  blocking collectives  96 us (13%)
  between operations  14.4 us (2%)
    all_gather x2, waiting for transfers between devices, prefix(): pieces = jax.tree.map(lambda part: lax.all_gather(part, axis), value)  187 us
    all_gather x1, blocking collectives, prefix(): pieces = jax.tree.map(lambda part: lax.all_gather(part, axis), value)  96 us
    select_n x62, other arithmetic, step(): jnp.where(position < mine, new, old)  73.1 us
    dot_general x12, matrix products, block_step(): within = jnp.einsum('hts,shp->thp', mixing, x_block, precision=highest)  47 us
    dynamic_update_slice x24, other arithmetic, scan_blocks(): lax.scan(stepper, start, (x_blocks, b_blocks, c_blocks, rate_blocks, step...  26.9 us
    dynamic_slice x20, local copies, waits for them, and re-layouts, scan_blocks(): lax.scan(stepper, start, (x_blocks, b_blocks, c_blocks, rate_blocks, step...  25.7 us
    dot_general x12, matrix products, block_step(): jnp.einsum('thn,hpn->thp', c_heads, carried, precision=highest)  25.6 us
    dot_general x12, matrix products, block_step(): jnp.einsum('sh,shp,shn->hpn', weighted, x_block, b_heads, precision=highest)  25.3 us
  transfers between devices with their start and end apart: 5, of which 4 were waited for; matrix products, arithmetic and copies ran while one was open for 51% of the time, Pallas kernels for 0%

commit v1 on v0

v1 whole, which is shorter than its diff:
```python
import functools

import jax
import jax.numpy as jnp
from jax import lax
from jax.experimental import pallas as pl
from jax.experimental.pallas import tpu as pltpu
from jax.sharding import PartitionSpec as P

T = 512
N = 128
HP = 1024
H = 16
NB = T // N
NP = HP // N
SEQ = 32

f32 = jnp.float32
bf16 = jnp.bfloat16
HI = lax.Precision.HIGHEST
NN = (((1,), (0,)), ((), ()))
NT = (((1,), (1,)), ((), ()))
TN = (((0,), (0,)), ((), ()))
OFF = -1e30


def dot(a, b, dims=NN, precision=None):
    return lax.dot_general(a, b, dims, precision=precision, preferred_element_type=f32)


def iota(shape, axis):
    return lax.broadcasted_iota(jnp.int32, shape, axis)


def pair_of(ref, rows, j, count):
    first = jnp.broadcast_to(ref[rows, 2 * j : 2 * j + 1], (count, N))
    second = jnp.broadcast_to(ref[rows, 2 * j + 1 : 2 * j + 2], (count, N))
    return jnp.where(iota((count, N), 1) < 64, first, second), first, second


def head_rows():
    row, col = iota((H, HP), 0), iota((H, HP), 1)
    return ((col >= 64 * row) & (col < 64 * row + 64)).astype(bf16)


def halves(value):
    high = value.astype(bf16)
    return high, (value - high.astype(f32)).astype(bf16)


def head_sums(value):
    high, low = halves(value)
    ones = head_rows()
    return dot(ones, high, NT) + dot(ones, low, NT)


def stacked(value):
    low = iota(value.shape, 1) < 64
    zero = jnp.zeros_like(value)
    return jnp.concatenate([jnp.where(low, value, zero), jnp.where(low, zero, value)], axis=0)


def lanes(j):
    return slice(N * j, N * j + N)


def prepare(dt, bias, alog, step, r, step_t, r_t):
    raw = dt[...] + bias[...]
    step[...] = jnp.maximum(raw, 0.0) + jnp.log1p(jnp.exp(-jnp.abs(raw)))
    rate = -step[...] * jnp.exp(alog[...])
    row, col = iota((N, N), 0), iota((N, N), 1)
    upper = (row <= col).astype(f32)
    eye = (row == col).astype(f32)
    for b in range(NB):
        at = lanes(b)
        r[:, at] = dot(rate[:, at], upper, precision=HI)
        r_t[at, :] = dot(eye, r[:, at], NT, HI)
        step_t[at, :] = dot(eye, step[:, at], NT, HI)


def forward_block(b, x, bm, cm, r, r_t, step_t, keep_t, within, er, xw, sl, pd, st):
    base = pl.multiple_of(b * N, N)
    rows = pl.ds(base, N)
    mask = iota((N, N), 0) >= iota((N, N), 1)
    b_blk, c_blk = bm[rows, :], cm[rows, :]
    b_flip = b_blk.astype(f32).T.astype(bf16)
    scores = dot(c_blk, b_blk, NT)
    for j in range(NP):
        at = lanes(j)
        run, run0, run1 = pair_of(r_t, rows, j, N)
        size = pair_of(step_t, rows, j, N)[0]
        last = pair_of(r_t, pl.ds(base + N - 1, 1), j, 1)[0]
        keep = pair_of(keep_t.at[b], slice(0, 1), j, 1)[0]
        mixing = [
            (jnp.exp(jnp.where(mask, col - r[2 * j + k : 2 * j + k + 1, rows], OFF)) * scores).astype(bf16)
            for k, col in enumerate((run0, run1))
        ]
        x_val = x[rows, at].astype(f32)
        sized = x_val * size
        within[rows, at] = dot(jnp.concatenate(mixing, axis=1), stacked(sized.astype(bf16)))
        er[rows, at] = jnp.exp(run)
        weighted = (sized * jnp.exp(last - run)).astype(bf16)
        xw[rows, at] = weighted
        state = st[:, at] * keep
        sl[b, :, at] = state
        span = pd[b, :, at] * keep
        pd[b, :, at] = span
        decay = jnp.exp(last)
        pd[b + 1, :, at] = span * decay
        st[:, at] = state * decay + dot(b_flip, weighted)


def forward_local(*refs):
    sl, pd, st = refs[-3:]
    st[...] = jnp.zeros_like(st)
    pd[0] = jnp.ones((1, HP), f32)

    def step(b, carry):
        forward_block(b, *refs)
        return carry

    lax.fori_loop(0, NB, step, 0)
    sl[NB] = st[...]


def enter(x, cm, sl, pd, entering, er, skip, within, y, sin):
    def step(b, carry):
        rows = pl.ds(pl.multiple_of(b * N, N), N)
        c_blk = cm[rows, :]
        for j in range(NP):
            at = lanes(j)
            state = sl[b, :, at] + pd[b, :, at] * entering[:, at]
            sin[b, :, at] = state
            high, low = halves(state)
            y[rows, at] = within[rows, at] + (dot(c_blk, high) + dot(c_blk, low)) * er[rows, at] + skip[:, at] * x[rows, at].astype(f32)
        return carry

    lax.fori_loop(0, NB, step, 0)


CH = 32


def norm(y, z, gain, normed):
    def step(i, carry):
        rows = pl.ds(pl.multiple_of(i * CH, CH), CH)
        z_val = z[rows, :].astype(f32)
        gated = y[rows, :] * (z_val / (1.0 + jnp.exp(-z_val)))
        factor = lax.rsqrt(jnp.mean(gated * gated, axis=1, keepdims=True) + 1e-05)
        normed[rows, :] = (gated * factor * gain[...]).astype(bf16)
        return carry

    lax.fori_loop(0, T // CH, step, 0)


def unnorm(y, within, x, z, gain, skip, d_normed, d_z, d_y, work, carried):
    def step(i, carry):
        rows = pl.ds(pl.multiple_of(i * CH, CH), CH)
        z_val = z[rows, :].astype(f32)
        y_val = y[rows, :]
        sig = 1.0 / (1.0 + jnp.exp(-z_val))
        silu = z_val * sig
        gated = y_val * silu
        factor = lax.rsqrt(jnp.mean(gated * gated, axis=1, keepdims=True) + 1e-05)
        scaled = d_normed[rows, :] * gain[...]
        along = jnp.mean(scaled * gated, axis=1, keepdims=True)
        d_gated = factor * scaled - gated * (factor * factor * factor * along)
        d_z[rows, :] = (d_gated * y_val * (sig * (1.0 + z_val * (1.0 - sig)))).astype(bf16)
        d_mixed = d_gated * silu
        d_y[rows, :] = d_mixed
        own = within[rows, :]
        work[rows, :] = d_mixed * own
        carried[rows, :] = d_mixed * (y_val - skip[...] * x[rows, :].astype(f32) - own)
        return carry

    lax.fori_loop(0, T // CH, step, 0)


def gather_heads(work, sums):
    def step(b, carry):
        rows = pl.ds(pl.multiple_of(b * N, N), N)
        sums[:, rows] = head_sums(work[rows, :])
        return carry

    lax.fori_loop(0, NB, step, 0)


def state_grad(cm, r_t, keep_t, er, d_y, erdy, gl, qd, gt):
    gt[...] = jnp.zeros_like(gt)
    qd[NB - 1] = jnp.ones((1, HP), f32)

    def step(i, carry):
        b = NB - 1 - i
        base = pl.multiple_of(b * N, N)
        rows = pl.ds(base, N)
        c_flip = cm[rows, :].astype(f32).T.astype(bf16)
        for j in range(NP):
            at = lanes(j)
            last = pair_of(r_t, pl.ds(base + N - 1, 1), j, 1)[0]
            keep = pair_of(keep_t.at[b], slice(0, 1), j, 1)[0]
            high, low = halves(er[rows, at] * d_y[rows, at])
            erdy[0, rows, at] = high
            erdy[1, rows, at] = low
            grad = gt[:, at]
            gl[b, :, at] = grad
            decay = jnp.exp(last)
            gt[:, at] = keep * (decay * grad + dot(c_flip, high) + dot(c_flip, low))
            value = qd[b, :, at]

            @pl.when(b > 0)
            def _():
                qd[b - 1, :, at] = keep * decay * value

        return carry

    lax.fori_loop(0, NB, step, 0)


def backward_within(x, bm, cm, r, r_t, step_t, d_y, v, ds):
    def step(b, carry):
        rows = pl.ds(pl.multiple_of(b * N, N), N)
        mask = iota((N, N), 0) <= iota((N, N), 1)
        scores = dot(bm[rows, :], cm[rows, :], NT)
        total = jnp.zeros((N, N), f32)
        for j in range(NP):
            at = lanes(j)
            run0 = jnp.broadcast_to(r_t[rows, 2 * j : 2 * j + 1], (N, N))
            run1 = jnp.broadcast_to(r_t[rows, 2 * j + 1 : 2 * j + 2], (N, N))
            size = pair_of(step_t, rows, j, N)[0]
            decays = [
                jnp.exp(jnp.where(mask, r[2 * j + k : 2 * j + k + 1, rows] - col, OFF))
                for k, col in enumerate((run0, run1))
            ]
            high, low = halves(d_y[rows, at])
            mixing = jnp.concatenate([(decay * scores).astype(bf16) for decay in decays], axis=1)
            v[rows, at] = dot(mixing, stacked(high)) + dot(mixing, stacked(low))
            sized = (x[rows, at].astype(f32) * size).astype(bf16)
            both = stacked(sized)
            product = dot(both, high, NT) + dot(both, low, NT)
            total = total + product[:N] * decays[0] + product[N:] * decays[1]
        ds[b] = total.astype(bf16)
        return carry

    lax.fori_loop(0, NB, step, 0)


def backward_rest(x, bm, cm, r_t, step_t, skip, d_y, v, ds, xw, erdy, sin, gl, qd, arriving, ge, psi, own, d_x, d_b, d_c):
    def step(b, carry):
        base = pl.multiple_of(b * N, N)
        rows = pl.ds(base, N)
        b_blk, c_blk = bm[rows, :], cm[rows, :]
        for j in range(NP):
            at = lanes(j)
            run = pair_of(r_t, rows, j, N)[0]
            size = pair_of(step_t, rows, j, N)[0]
            last = pair_of(r_t, pl.ds(base + N - 1, 1), j, 1)[0]
            grad = gl[b, :, at] + qd[b, :, at] * arriving[:, at]
            passing = grad * sin[b, :, at]
            psi[b, :, at] = jnp.exp(last) * jnp.sum(passing.reshape(N // 8, 8, N), axis=0)
            high, low = halves(grad)
            ge[0, :, at] = high
            ge[1, :, at] = low
            local = v[rows, at]
            reach = dot(b_blk, high) + dot(b_blk, low)
            carried = jnp.exp(last - run) * reach
            x_val = x[rows, at].astype(f32)
            sized = x_val * size
            d_x[rows, at] = (size * (local + carried) + skip[:, at] * d_y[rows, at]).astype(bf16)
            own[rows, at] = sized.astype(bf16).astype(f32) * local
            v[rows, at] = xw[rows, at].astype(f32) * reach
            d_y[rows, at] = x_val * (local + carried)
        d_b[rows, :] = (dot(ds[b], c_blk) + dot(xw[rows, :], ge[0], NT) + dot(xw[rows, :], ge[1], NT)).astype(bf16)
        late = sin[b].astype(bf16)
        d_c[rows, :] = (dot(ds[b], b_blk, TN) + dot(erdy[0, rows, :], late, NT) + dot(erdy[1, rows, :], late, NT)).astype(bf16)
        return carry

    lax.fori_loop(0, NB, step, 0)


def steps_grad(dt, bias, alog, step, psi, row_own, row_carried, own, carried, whole, out):
    row, col = iota((N, N), 0), iota((N, N), 1)
    since = (row >= col).astype(f32)
    before = (row < col).astype(f32)
    raw = dt[...] + bias[...]
    sig = 1.0 / (1.0 + jnp.exp(-raw))
    pull = jnp.exp(alog[...])
    ones = head_rows().astype(f32)
    for b in range(NB):
        at = lanes(b)
        past = jnp.sum(dot(ones, psi[b], NT, HI), axis=1, keepdims=True)
        d_rate = dot(row_own[:, at] - own[:, at] + row_carried[:, at], since, precision=HI) + past
        d_rate = d_rate + dot(carried[:, at], before, precision=HI)
        out[:, at] = (whole[:, at] - pull * d_rate) * sig[:, at]
MESH = pl.DeviceIdType.MESH
SHARD = 128
HALF = HP // 2
D = 4096


def mod(value, size):
    return lax.rem(value + size, size)


def greet(seqs, heads):
    barrier = pltpu.get_barrier_semaphore()
    for s in seqs:
        pl.semaphore_signal(barrier, inc=1, device_id={"seq": s}, device_id_type=MESH)
    for h in heads:
        pl.semaphore_signal(barrier, inc=1, device_id={"head": h}, device_id_type=MESH)
    pl.semaphore_wait(barrier, len(seqs) + len(heads))


def greet_all(me):
    barrier = pltpu.get_barrier_semaphore()

    def step(k, carry):
        pl.semaphore_signal(barrier, inc=1, device_id={"seq": lax.rem(me + k, SEQ)}, device_id_type=MESH)
        return carry

    lax.fori_loop(1, SEQ, step, 0)
    pl.semaphore_wait(barrier, SEQ - 1)


def remote(src, dst, ssem, rsem, **device):
    return pltpu.make_async_remote_copy(
        src_ref=src, dst_ref=dst, send_sem=ssem, recv_sem=rsem, device_id=device, device_id_type=MESH
    )


SLICE = 32


def each_other(me, fn):
    def step(k, carry):
        fn(lax.rem(me + k, SEQ))
        return carry

    lax.fori_loop(1, SEQ, step, 0)


def to_copy(me, buf, land, ssem, rsem, other):
    return remote(buf.at[other], land.at[me], ssem.at[other], rsem.at[me], seq=other)


def from_copy(me, buf, land, ssem, rsem, other):
    return remote(buf.at[me], land.at[other], ssem.at[me], rsem.at[other], seq=other)


def exchange_out(me, state, decay, out1, in1, s1, r1):
    for j in range(NP):
        for i in range(N // SLICE):
            k = j * (N // SLICE) + i
            out1[k, :SLICE] = state[SLICE * i : SLICE * (i + 1), lanes(j)]
            out1[k, SLICE:] = jnp.broadcast_to(decay[:, lanes(j)], (8, N))
    each_other(me, lambda o: to_copy(me, out1, in1, s1, r1, o).start())
    in1[me] = out1[me]


def exchange_fold(me, backward, out1, in1, s1, r1, out2, in2, s2, r2):
    each_other(me, lambda o: from_copy(me, out1, in1, s1, r1, o).wait_recv())

    def step(i, total):
        at = SEQ - 1 - i if backward else i
        out2[at] = total
        return total * in1[at, SLICE : SLICE + 1] + in1[at, :SLICE]

    lax.fori_loop(0, SEQ, step, jnp.zeros((SLICE, N), f32))
    each_other(me, lambda o: to_copy(me, out2, in2, s2, r2, o).start())
    in2[me] = out2[me]


def exchange_in(me, result, out1, in1, s1, r1, out2, in2, s2, r2):
    each_other(me, lambda o: from_copy(me, out2, in2, s2, r2, o).wait_recv())
    for j in range(NP):
        for i in range(N // SLICE):
            result[SLICE * i : SLICE * (i + 1), lanes(j)] = in2[j * (N // SLICE) + i]

    def done(o):
        to_copy(me, out1, in1, s1, r1, o).wait_send()
        to_copy(me, out2, in2, s2, r2, o).wait_send()

    each_other(me, done)


EXCHANGE = [
    pltpu.VMEM((SEQ, SLICE + 8, N), f32),
    pltpu.VMEM((SEQ, SLICE + 8, N), f32),
    pltpu.SemaphoreType.DMA((SEQ,)),
    pltpu.SemaphoreType.DMA((SEQ,)),
    pltpu.VMEM((SEQ, SLICE, N), f32),
    pltpu.VMEM((SEQ, SLICE, N), f32),
    pltpu.SemaphoreType.DMA((SEQ,)),
    pltpu.SemaphoreType.DMA((SEQ,)),
]


class Torus:
    def __init__(self, half):
        self.half = half
        me = lax.axis_index("seq")
        x, y = lax.rem(me, 4), lax.rem(lax.div(me, 4), 4)
        self.z = lax.div(me, 16)
        self.p, self.q = (x, y) if half == 0 else (y, x)

    def at(self, z, p, q):
        return z * 16 + (q * 4 + p if self.half == 0 else p * 4 + q)

    def place(self, dz=0, dp=0, dq=0):
        z = 1 - self.z if dz else self.z
        return self.at(z, mod(self.p + dp, 4), mod(self.q + dq, 4))


def neighbours():
    t = Torus(0)
    return [t.place(dz=1), t.place(dp=1), t.place(dp=-1), t.place(dq=1), t.place(dq=-1)]


class Gather:
    def __init__(self, half, buf, ssem, rsem):
        self.t, self.half, self.buf, self.ssem, self.rsem, self.n = Torus(half), half, buf, ssem, rsem, 0
        self.sent = []

    def copy(self, shard, to, index):
        ref = self.buf.at[self.half, shard]
        return remote(ref, ref, self.ssem.at[self.half, index], self.rsem.at[self.half, shard], seq=to)

    def send(self, shard, to):
        copy = self.copy(shard, to, self.n)
        copy.start()
        self.sent.append(copy)
        self.n += 1

    def wait(self, shard):
        self.copy(shard, self.t.place(dz=1), 0).wait_recv()

    def spread(self, shard):
        self.send(shard, self.t.place(dq=1))
        self.send(shard, self.t.place(dq=-1))

    def own(self):
        t = self.t
        mine = t.place()
        self.send(mine, t.place(dz=1))
        self.send(mine, t.place(dp=1))
        self.send(mine, t.place(dp=-1))
        self.spread(mine)

    def across(self):
        t = self.t
        other = t.place(dz=1)
        self.wait(other)
        self.send(other, t.place(dp=1))
        self.send(other, t.place(dp=-1))
        self.spread(other)

    def near(self):
        t = self.t
        for z in (0, 1):
            for dp in (-1, 1):
                shard = t.at(z, mod(t.p + dp, 4), t.q)
                self.wait(shard)
                if (z, dp) in ((0, -1), (1, 1)):
                    self.send(shard, t.place(dp=-dp))
                self.spread(shard)

    def far(self):
        t = self.t
        for z in (0, 1):
            shard = t.at(z, mod(t.p + 2, 4), t.q)
            self.wait(shard)
            self.spread(shard)

    def pass_on(self):
        t = self.t
        for k in range(4):
            p = mod(t.p + (0, 1, 3, 2)[k], 4)
            for z, dq in ((0, -1), (1, 1)):
                shard = t.at(z, p, mod(t.q + dq, 4))
                self.wait(shard)
                self.send(shard, t.place(dq=-dq))

    def rest(self):
        t = self.t
        for p in range(4):
            for z, dq in ((1, -1), (0, 1), (0, 2), (1, 2)):
                self.wait(t.at(z, p, mod(t.q + dq, 4)))

    def close(self):
        for copy in self.sent:
            copy.wait_send()


class Heads:
    PARTS = 2

    def __init__(self, buf, ssem, rsem):
        self.h = lax.axis_index("head")
        self.core = self.h + 1 - 2 * lax.rem(self.h, 2)
        self.chip = lax.rem(self.h + 2, 4)
        self.buf, self.ssem, self.rsem, self.sent = buf, ssem, rsem, []

    def copy(self, block, part, to, index):
        ref = self.buf.at[block, pl.ds(part * (T // self.PARTS), T // self.PARTS)]
        return remote(ref, ref, self.ssem.at[index], self.rsem.at[block, part], head=to)

    def send(self, block, part, to):
        copy = self.copy(block, part, to, len(self.sent))
        copy.start()
        self.sent.append(copy)

    def own(self):
        for part in range(self.PARTS):
            self.send(self.h, part, self.chip)
        for part in range(self.PARTS):
            self.send(self.h, part, self.core)

    def across(self):
        for part in range(self.PARTS):
            self.copy(self.chip, part, self.chip, 0).wait_recv()
            self.send(self.chip, part, self.core)

    def rest(self):
        for part in range(self.PARTS):
            self.copy(self.core, part, self.core, 0).wait_recv()
            self.copy(lax.rem(self.core + 2, 4), part, self.core, 0).wait_recv()

    def close(self):
        for copy in self.sent:
            copy.wait_send()


FARP, FARM, NEARP, NEARM, PFARP, PFARM, PNEARP, PNEARM, ACROSS = 0, 4, 8, 16, 24, 25, 26, 28, 30
SLOTS = 31


class Scatter:
    def __init__(self, half, part, out, inn, ssem, rsem, acc, result):
        self.t, self.half, self.part, self.out, self.inn = Torus(half), half, part, out, inn
        self.ssem, self.rsem, self.acc, self.result = ssem, rsem, acc, result

    def copy(self, slot, to):
        h = self.half
        return remote(self.out.at[h, slot], self.inn.at[h, slot], self.ssem.at[h, slot], self.rsem.at[h, slot], seq=to)

    def send(self, slot, value, to):
        self.out[self.half, slot] = value.astype(bf16)
        self.copy(slot, to).start()

    def got(self, slot):
        self.copy(slot, self.t.place(dz=1)).wait_recv()
        return self.inn[self.half, slot].astype(f32)

    def loop(self, fn):
        def step(p, carry):
            fn(p)
            return carry

        lax.fori_loop(0, 4, step, 0)

    def q_far(self):
        t = self.t
        far = mod(t.q + 2, 4)

        def fn(p):
            self.send(FARP + p, self.part(self.half, t.at(0, p, far)), t.place(dq=1))
            self.send(FARM + p, self.part(self.half, t.at(1, p, far)), t.place(dq=-1))

        self.loop(fn)

    def q_near(self):
        t = self.t
        up, down = mod(t.q + 1, 4), mod(t.q - 1, 4)

        def fn(p):
            self.send(NEARP + 4 + p, self.part(self.half, t.at(1, p, up)), t.place(dq=1))
            self.send(NEARM + p, self.part(self.half, t.at(0, p, down)), t.place(dq=-1))

        self.loop(fn)

    def q_pass(self):
        t = self.t
        up, down = mod(t.q + 1, 4), mod(t.q - 1, 4)

        def fn(p):
            self.send(NEARP + p, self.part(self.half, t.at(0, p, up)) + self.got(FARP + p), t.place(dq=1))
            self.send(NEARM + 4 + p, self.part(self.half, t.at(1, p, down)) + self.got(FARM + p), t.place(dq=-1))

        self.loop(fn)

    def q_own(self):
        t = self.t

        def fn(p):
            for z in (0, 1):
                self.acc[self.half, z, p] = self.part(self.half, t.at(z, p, t.q))

        self.loop(fn)

    def total(self, z, p):
        return self.acc[self.half, z, p] + self.got(NEARP + 4 * z + p) + self.got(NEARM + 4 * z + p)

    def p_far(self):
        t = self.t
        far = mod(t.p + 2, 4)
        self.send(PFARP, self.total(0, far), t.place(dp=1))
        self.send(PFARM, self.total(1, far), t.place(dp=-1))

    def p_near(self):
        t = self.t
        up, down = mod(t.p + 1, 4), mod(t.p - 1, 4)
        self.send(PNEARP + 1, self.total(1, up), t.place(dp=1))
        self.send(PNEARM, self.total(0, down), t.place(dp=-1))
        self.send(PNEARP, self.total(0, up) + self.got(PFARP), t.place(dp=1))
        self.send(PNEARM + 1, self.total(1, down) + self.got(PFARM), t.place(dp=-1))

    def p_own(self):
        t = self.t
        for z in (0, 1):
            self.acc[self.half, z, t.p] = self.total(z, t.p)

    def p_sum(self, z):
        return self.acc[self.half, z, self.t.p] + self.got_at(PNEARP, z) + self.got_at(PNEARM, z)

    def got_at(self, base, z):
        return self.got(base + z)

    def z_out(self):
        t = self.t
        self.send(ACROSS, self.p_sum(1 - t.z), t.place(dz=1))

    def z_in(self):
        t = self.t
        self.result[:, HALF * self.half : HALF * (self.half + 1)] = self.p_sum(t.z) + self.got(ACROSS)

    def close(self):
        def step(slot, carry):
            self.copy(slot, self.t.place(dz=1)).wait_send()
            return carry

        lax.fori_loop(0, SLOTS, step, 0)


V = pltpu.VMEM
DMA = pltpu.SemaphoreType.DMA


def call(fn, outs, scratch, *args, cid=None):
    return pl.pallas_call(
        fn,
        out_shape=[jax.ShapeDtypeStruct(s, d) for s, d in outs],
        in_specs=[pl.BlockSpec(memory_space=pltpu.VMEM)] * len(args),
        out_specs=[pl.BlockSpec(memory_space=pltpu.VMEM)] * len(outs),
        scratch_shapes=scratch,
        compiler_params=pltpu.CompilerParams(vmem_limit_bytes=60 << 20, collective_id=cid, has_side_effects=cid is not None),
    )(*args)


def k1(x, bm, cm, dt, bias, alog, keep_t, within, er, xw, sl, pd, step, r, step_t, r_t, st):
    prepare(dt, bias, alog, step, r, step_t, r_t)
    forward_local(x, bm, cm, r, r_t, step_t, keep_t, within, er, xw, sl, pd, st)


def k2(x, cm, sl, pd, entering, er, skip, within, z, gain, y, sin, normed):
    enter(x, cm, sl, pd, entering, er, skip, within, y, sin)
    norm(y, z, gain, normed)


def k3(y, within, x, z, gain, skip, d_normed, cm, r_t, keep_t, er, d_z, d_y, row_own, row_carried, erdy, gl, qd, gt, work, carried):
    unnorm(y, within, x, z, gain, skip, d_normed, d_z, d_y, work, carried)
    gather_heads(work, row_own)
    gather_heads(carried, row_carried)
    state_grad(cm, r_t, keep_t, er, d_y, erdy, gl, qd, gt)


def k4(x, bm, cm, r, r_t, step_t, skip, d_y0, xw, erdy, sin, gl, qd, arriving,
       dt, bias, alog, step, row_own, row_carried, d_x, d_b, d_c, out, d_y, v, ds, ge, psi, own, s1, s2, s3):
    d_y[...] = d_y0[...]
    backward_within(x, bm, cm, r, r_t, step_t, d_y, v, ds)
    backward_rest(x, bm, cm, r_t, step_t, skip, d_y, v, ds, xw, erdy, sin, gl, qd, arriving, ge, psi, own, d_x, d_b, d_c)
    gather_heads(own, s1)
    gather_heads(v, s2)
    gather_heads(d_y, s3)
    steps_grad(dt, bias, alog, step, psi, row_own, row_carried, s1, s2, s3, out)


def kx(backward, state, decay, result, *bufs):
    me = lax.axis_index("seq")
    greet_all(me)
    exchange_out(me, state, decay, *bufs[:4])
    exchange_fold(me, backward, *bufs)
    exchange_in(me, result, *bufs)


def multiply(cots, ws, out):
    def step(i, carry):
        half, tile = lax.div(i, 2), lax.rem(i, 2)
        at = pl.ds(pl.multiple_of(tile * 256, 256), 256)
        total = None
        for k in range(4):
            rows = ws[half, 8 * k : 8 * k + 8, :, at].reshape(1024, 256)
            term = dot(cots[k], rows)
            total = term if total is None else total + term
        out[:, pl.ds(pl.multiple_of(i * 256, 256), 256)] = total
        return carry

    lax.fori_loop(0, 4, step, 0)


def kg(w, cot, d_normed, cots, wbuf, cbuf, ws, wr, cs, cr):
    heads = Heads(cbuf, cs, cr)
    gathers = [Gather(h, wbuf, ws, wr) for h in (0, 1)]
    me = lax.axis_index("seq")
    wbuf[0, me] = w[:, :HALF]
    wbuf[1, me] = w[:, HALF:]
    cbuf[heads.h] = cot[...]
    greet(neighbours(), [heads.core, heads.chip])
    for name in ("own", "across", "near", "far", "pass_on", "rest"):
        for g in gathers:
            getattr(g, name)()
        if name in ("own", "across", "rest"):
            getattr(heads, name)()
    multiply(cbuf, wbuf, d_normed)
    cots[...] = cbuf[...]
    for g in gathers:
        g.close()
    heads.close()


def ks(cots, normed, result, out, inn, ss, rs, acc):
    def part(half, shard):
        block, at = lax.div(shard, 8), lax.rem(shard, 8)
        cols = pl.ds(pl.multiple_of(at * SHARD, SHARD), SHARD)
        return dot(cots[block, :, cols], normed[:, HALF * half : HALF * (half + 1)], TN)

    greet(neighbours(), [])
    scatters = [Scatter(h, part, out, inn, ss, rs, acc, result) for h in (0, 1)]
    for name in ("q_far", "q_near", "q_pass", "q_own", "p_far", "p_near", "p_own", "z_out", "z_in", "close"):
        for s in scatters:
            getattr(s, name)()


def body(x, z, bm, cm, dt, bias, alog, skip, gain, resets, w, cot):
    keep = 1.0 - resets.astype(f32)
    keep_t = keep.T[:, None, :]
    skip = jnp.repeat(skip, 64)[None]
    gain = gain[None]
    bias, alog = bias[:, None], alog[:, None]
    F, B = f32, bf16
    within, er, xw, sl, pd, step, r, step_t, r_t = call(
        k1, [((T, HP), F), ((T, HP), F), ((T, HP), B), ((NB + 1, N, HP), F), ((NB + 1, 1, HP), F), ((H, T), F), ((H, T), F), ((T, H), F), ((T, H), F)],
        [V((N, HP), F)], x, bm, cm, dt, bias, alog, keep_t)
    entering = call(functools.partial(kx, False), [((N, HP), F)], EXCHANGE, sl[NB], pd[NB], cid=0)[0]
    y, sin, normed = call(k2, [((T, HP), F), ((NB, N, HP), F), ((T, HP), B)], [], x, cm, sl, pd, entering, er, skip, within, z, gain)
    d_normed, cots = call(
        kg, [((T, HP), F), ((4, T, HP), B)],
        [V((2, SEQ, SHARD, HALF), B), V((4, T, HP), B), DMA((2, 31)), DMA((2, SEQ)), DMA((6,)), DMA((4, 2))], w, cot, cid=2)
    d_z, d_y, row_own, row_carried, erdy, gl, qd, gt = call(
        k3, [((T, HP), B), ((T, HP), F), ((H, T), F), ((H, T), F), ((2, T, HP), B), ((NB, N, HP), F), ((NB + 1, 1, HP), F), ((N, HP), F)],
        [V((T, HP), F), V((T, HP), F)], y, within, x, z, gain, skip, d_normed, cm, r_t, keep_t, er)
    arriving = call(functools.partial(kx, True), [((N, HP), F)], EXCHANGE, gt, pd[NB], cid=1)[0]
    d_x, d_b, d_c, out = call(
        k4, [((T, HP), B), ((T, N), B), ((T, N), B), ((H, T), F)],
        [V((T, HP), F), V((T, HP), F), V((NB, N, N), B), V((2, N, HP), B), V((NB, 8, HP), F), V((T, HP), F), V((H, T), F), V((H, T), F), V((H, T), F)],
        x, bm, cm, r, r_t, step_t, skip, d_y, xw, erdy, sin, gl, qd, arriving, dt, bias, alog, step, row_own, row_carried)
    d_w = call(
        ks, [((SHARD, HP), F)],
        [V((2, SLOTS, SHARD, HALF), B), V((2, SLOTS, SHARD, HALF), B), DMA((2, SLOTS)), DMA((2, SLOTS)), V((2, 2, 4, SHARD, HALF), F)],
        cots, normed, cid=3)[0]
    return d_x, d_z, d_b, d_c, out, d_w


def solution(mesh):
    s, h = P("seq", "head"), P("head")
    return jax.shard_map(
        body, mesh=mesh,
        in_specs=(s, s, s, s, P("head", "seq"), h, h, h, h, P("head", "seq"), s, s),
        out_specs=(s, s, s, s, P("head", "seq"), s), check_vma=False)
```

time: 749 us -> 253 us (0.34); the launches traced: 738 us -> 252 us
  Pallas kernels: 0 us -> 242 us
  waiting for transfers between devices: 213 us -> 0 us
  other arithmetic: 151 us -> 1.26 us
  matrix products: 131 us -> 0 us
  local copies, waits for them, and re-layouts: 131 us -> 8 us
  blocking collectives: 96 us -> 0 us
  between operations: 14.4 us -> 0.68 us
    pallas_call x0 -> x8, Pallas kernels: none -> 242 us  [call(): pl.pallas_call(fn, out_shape=[jax.ShapeDtypeStruct(s, d) for s, d in outs...]
    all_gather x4 -> x0, waiting for transfers between devices: 209 us -> none  [the longest x2 187 us: prefix(): pieces = jax.tree.map(lambda part: lax.all_gather(part, axis), value)]
    dot_general x52 -> x0, matrix products: 131 us -> none  [the longest x12 47 us: block_step(): within = jnp.einsum('hts,shp->thp', mixing, x_block, precision=highest)]
    all_gather x1 -> x0, blocking collectives: 96 us -> none  [prefix(): pieces = jax.tree.map(lambda part: lax.all_gather(part, axis), value)]
    select_n x63 -> x0, other arithmetic: 74 us -> none  [the longest x62 73.1 us: step(): jnp.where(position < mine, new, old)]
    dynamic_update_slice x24 -> x0, other arithmetic: 26.9 us -> none  [scan_blocks(): lax.scan(stepper, start, (x_blocks, b_blocks, c_blocks, rate_blocks, step...]
    dynamic_slice x20 -> x0, local copies, waits for them, and re-layouts: 25.7 us -> none  [scan_blocks(): lax.scan(stepper, start, (x_blocks, b_blocks, c_blocks, rate_blocks, step...]
    reduce_sum x16 -> x0, other arithmetic: 21.4 us -> none  [the longest x4 8.21 us: block_step(): weighted = (jnp.exp(running[:, -1:] - running) * step_block).T]
  transfers between devices with their start and end apart: 5 -> 0, of which waited for: 4 -> 0; matrix products, arithmetic and copies ran while one was open for 51% -> 0% of each run, Pallas kernels for 0% -> 0%
where the time goes in v1:
time: 253 us; the launch traced here: 252 us
  Pallas kernels  242 us (96%)
  local copies, waits for them, and re-layouts  8 us (3%)
    pallas_call x8, Pallas kernels, call(): pl.pallas_call(fn, out_shape=[jax.ShapeDtypeStruct(s, d) for s, d in outs...  242 us

profile of v1, /device:TPU:0, one launch (start us, length us, event | category | flops | bytes accessed | tf_op | source)
XLA Modules:
  0.0 252.3 jit_solution(1987472219459334228)
XLA Ops:
  0.6 1.3 convert_subtract_fusion
  1.9 1.3 copy.18.bias
  3.2 1.3 copy.19.alog
  4.5 0.7 broadcast_in_dim.18
  5.3 0.7 broadcast_in_dim_reshape.3.skip
  5.9 81.1 %shard_map.166 = (f32[512,1024]{1,0:T(8,128)}, bf16[4,512,1024]{2,1,0:T(8,128)(2,1)}) custom-call(bf16[128,1024]{1,0:T(8,128)(2,1)} %w.1, bf16[512,1024]{1,0:T(8,128)(2,1)} %cot.1), custom_call_target="tpu_custom_call" | custom-call | tf_op jit(solution)/shard_map/pallas_call | solution.py:648
  87.1 10.1 %shard_map.163 = (f32[512,1024]{1,0:T(8,128)}, f32[512,1024]{1,0:T(8,128)}, bf16[512,1024]{1,0:T(8,128)(2,1)}, f32[5,128,1024]{2,1,0:T(8,128)}, f32[5,1,1024]{2,...) custom-call(bf16[512,1024]{1,0:T(8,128)(2,1)} %x.7, ...), custom_call_target="tpu_custom_call" | custom-call | tf_op jit(solution)/shard_map/pallas_call | solution.py:648
  97.2 1.3 slice_bitcast_fusion.1.decay
  98.5 1.9 slice_bitcast_fusion.state
  100.4 23.3 %shard_map.164.entering = f32[128,1024]{1,0:T(8,128)} custom-call(f32[128,1024]{1,0:T(8,128)} %slice_bitcast_fusion.state, f32[1,1024]{1,0:T(1,128)} %slice_bitcast_fusion.1.decay), custom_call_target="tpu_custom_call" | custom-call | tf_op jit(solution)/shard_map/pallas_call | solution.py:648
  123.6 9.5 %shard_map.165 = (f32[512,1024]{1,0:T(8,128)}, f32[4,128,1024]{2,1,0:T(8,128)}, bf16[512,1024]{1,0:T(8,128)(2,1)}) custom-call(bf16[512,1024]{1,0:T(8,128)(2,1)} %x.7, bf16[512,128]{1,0:T(8,128)(2,1)} %cm.7, f32[5,128,1024]{2,1,0:T(8,128)} %get-tuple-element.35.sl, f32[5,1,1024]{2,1,0:T(1,128)} %get-tuple-element.36.pd, f32[128,1024]{1,0:T(8,128)} %shard_map.164.entering, ...), custom_call_target="tpu_custom_call" | custom-call | tf_op jit(solution)/shard_map/pallas_call | solution.py:648
  133.1 57.9 %shard_map.170 = f32[128,1024]{1,0:T(8,128)} custom-call(bf16[4,512,1024]{2,1,0:T(8,128)(2,1)} %get-tuple-element.56.cots, bf16[512,1024]{1,0:T(8,128)(2,1)} %get-tuple-element.57.normed), custom_call_target="tpu_custom_call" | custom-call | tf_op jit(solution)/shard_map/pallas_call | solution.py:648
  191.1 18.4 %shard_map.167 = (bf16[512,1024]{1,0:T(8,128)(2,1)}, f32[512,1024]{1,0:T(8,128)}, f32[16,512]{1,0:T(8,128)}, f32[16,512]{1,0:T(8,128)}, bf16[2,512,1024]{2,1,0:T...) custom-call(f32[512,1024]{1,0:T(8,128)} %get-tuple-element.39.y, ...), custom_call_target="tpu_custom_call" | custom-call | tf_op jit(solution)/shard_map/pallas_call | solution.py:648
  209.5 24.4 %shard_map.168.arriving = f32[128,1024]{1,0:T(8,128)} custom-call(f32[128,1024]{1,0:T(8,128)} %get-tuple-element.47.state, f32[1,1024]{1,0:T(1,128)} %slice_bitcast_fusion.1.decay), custom_call_target="tpu_custom_call" | custom-call | tf_op jit(solution)/shard_map/pallas_call | solution.py:648
  233.9 0.0 copy-start
  233.9 17.6 %shard_map.169 = (bf16[512,1024]{1,0:T(8,128)(2,1)}, bf16[512,128]{1,0:T(8,128)(2,1)}, bf16[512,128]{1,0:T(8,128)(2,1)}, f32[16,512]{1,0:T(8,128)}) custom-call(bf16[512,1024]{1,0:T(8,128)(2,1)} %x.7, bf16[512,128]{1,0:T(8,128)(2,1)} %bm.3, bf16[512,128]{1,0:T(8,128)(2,1)} %cm.7, f32[16,512]{1,0:T(8,128)} %get-tuple-element.32.r, ...), custom_call_target="tpu_custom_call" | custom-call | tf_op jit(solution)/shard_map/pallas_call | solution.py:648
  251.5 0.0 copy-done
  251.5 0.8 copy.25
Async XLA Ops:
  233.9 17.6 %copy-start = (f32[128,1024]{1,0:T(8,128)S(1)}, f32[128,1024]{1,0:T(8,128)}, u32[]{:S(2)}) copy-start(f32[128,1024]{1,0:T(8,128)} %shard_map.170) | copy-start | bytes 1572868

commit v2 on v1

--- a/solution.py
+++ b/solution.py
@@ -1,5 +1,3 @@
-import functools
-
 import jax
 import jax.numpy as jnp
 from jax import lax
@@ -64,10 +62,22 @@
     return slice(N * j, N * j + N)
 
 
-def prepare(dt, bias, alog, step, r, step_t, r_t):
-    raw = dt[...] + bias[...]
+def column(ref):
+    eye = iota((H, H), 0) == iota((H, H), 1)
+    return jnp.sum(jnp.where(eye, jnp.broadcast_to(ref[...], (H, H)), 0.0), axis=1, keepdims=True)
+
+
+def prepare(dt, bias, alog, resets, skip, step, r, step_t, r_t, keep_t, skips):
+    raw = dt[...] + column(bias)
     step[...] = jnp.maximum(raw, 0.0) + jnp.log1p(jnp.exp(-jnp.abs(raw)))
-    rate = -step[...] * jnp.exp(alog[...])
+    rate = -step[...] * jnp.exp(column(alog))
+    keep = 1.0 - resets[...].astype(f32)
+    square = iota((H, H), 0) == iota((H, H), 1)
+    for b in range(NB):
+        spread = jnp.where(square, jnp.broadcast_to(keep[:, b : b + 1], (H, H)), 0.0)
+        keep_t[b] = jnp.sum(spread, axis=0, keepdims=True)
+    for j in range(NP):
+        skips[:, lanes(j)] = pair_of(skip, slice(0, 1), j, 1)[0]
     row, col = iota((N, N), 0), iota((N, N), 1)
     upper = (row <= col).astype(f32)
     eye = (row == col).astype(f32)
@@ -79,7 +89,7 @@
 
 
 def forward_block(b, x, bm, cm, r, r_t, step_t, keep_t, within, er, xw, sl, pd, st):
-    base = pl.multiple_of(b * N, N)
+    base = b * N
     rows = pl.ds(base, N)
     mask = iota((N, N), 0) >= iota((N, N), 1)
     b_blk, c_blk = bm[rows, :], cm[rows, :]
@@ -110,27 +120,19 @@
         st[:, at] = state * decay + dot(b_flip, weighted)
 
 
-def forward_local(*refs):
-    sl, pd, st = refs[-3:]
+def forward_start(pd, st):
     st[...] = jnp.zeros_like(st)
     pd[0] = jnp.ones((1, HP), f32)
 
-    def step(b, carry):
-        forward_block(b, *refs)
-        return carry
-
-    lax.fori_loop(0, NB, step, 0)
-    sl[NB] = st[...]
-
-
-def enter(x, cm, sl, pd, entering, er, skip, within, y, sin):
+
+def enter(x, cm, sl, pd, entering, er, skip, within, y):
     def step(b, carry):
         rows = pl.ds(pl.multiple_of(b * N, N), N)
         c_blk = cm[rows, :]
         for j in range(NP):
             at = lanes(j)
             state = sl[b, :, at] + pd[b, :, at] * entering[:, at]
-            sin[b, :, at] = state
+            sl[b, :, at] = state
             high, low = halves(state)
             y[rows, at] = within[rows, at] + (dot(c_blk, high) + dot(c_blk, low)) * er[rows, at] + skip[:, at] * x[rows, at].astype(f32)
         return carry
@@ -153,7 +155,7 @@
     lax.fori_loop(0, T // CH, step, 0)
 
 
-def unnorm(y, within, x, z, gain, skip, d_normed, d_z, d_y, work, carried):
+def unnorm(y, within, x, z, gain, skip, d_normed, d_z, d_y):
     def step(i, carry):
         rows = pl.ds(pl.multiple_of(i * CH, CH), CH)
         z_val = z[rows, :].astype(f32)
@@ -169,8 +171,8 @@
         d_mixed = d_gated * silu
         d_y[rows, :] = d_mixed
         own = within[rows, :]
-        work[rows, :] = d_mixed * own
-        carried[rows, :] = d_mixed * (y_val - skip[...] * x[rows, :].astype(f32) - own)
+        y[rows, :] = d_mixed * own
+        d_normed[rows, :] = d_mixed * (y_val - skip[...] * x[rows, :].astype(f32) - own)
         return carry
 
     lax.fori_loop(0, T // CH, step, 0)
@@ -185,7 +187,7 @@
     lax.fori_loop(0, NB, step, 0)
 
 
-def state_grad(cm, r_t, keep_t, er, d_y, erdy, gl, qd, gt):
+def state_grad(cm, r_t, keep_t, er, d_y, gl, qd, gt):
     gt[...] = jnp.zeros_like(gt)
     qd[NB - 1] = jnp.ones((1, HP), f32)
 
@@ -199,8 +201,6 @@
             last = pair_of(r_t, pl.ds(base + N - 1, 1), j, 1)[0]
             keep = pair_of(keep_t.at[b], slice(0, 1), j, 1)[0]
             high, low = halves(er[rows, at] * d_y[rows, at])
-            erdy[0, rows, at] = high
-            erdy[1, rows, at] = low
             grad = gt[:, at]
             gl[b, :, at] = grad
             decay = jnp.exp(last)
@@ -244,7 +244,7 @@
     lax.fori_loop(0, NB, step, 0)
 
 
-def backward_rest(x, bm, cm, r_t, step_t, skip, d_y, v, ds, xw, erdy, sin, gl, qd, arriving, ge, psi, own, d_x, d_b, d_c):
+def backward_rest(x, bm, cm, r_t, step_t, skip, d_y, v, ds, xw, er, sl, gl, qd, arriving, ge, gy, psi, own, d_x, d_b, d_c):
     def step(b, carry):
         base = pl.multiple_of(b * N, N)
         rows = pl.ds(base, N)
@@ -255,12 +255,13 @@
             size = pair_of(step_t, rows, j, N)[0]
             last = pair_of(r_t, pl.ds(base + N - 1, 1), j, 1)[0]
             grad = gl[b, :, at] + qd[b, :, at] * arriving[:, at]
-            passing = grad * sin[b, :, at]
+            passing = grad * sl[b, :, at]
             psi[b, :, at] = jnp.exp(last) * jnp.sum(passing.reshape(N // 8, 8, N), axis=0)
             high, low = halves(grad)
             ge[0, :, at] = high
             ge[1, :, at] = low
             local = v[rows, at]
+            gy[0, :, at], gy[1, :, at] = halves(er[rows, at] * d_y[rows, at])
             reach = dot(b_blk, high) + dot(b_blk, low)
             carried = jnp.exp(last - run) * reach
             x_val = x[rows, at].astype(f32)
@@ -270,8 +271,8 @@
             v[rows, at] = xw[rows, at].astype(f32) * reach
             d_y[rows, at] = x_val * (local + carried)
         d_b[rows, :] = (dot(ds[b], c_blk) + dot(xw[rows, :], ge[0], NT) + dot(xw[rows, :], ge[1], NT)).astype(bf16)
-        late = sin[b].astype(bf16)
-        d_c[rows, :] = (dot(ds[b], b_blk, TN) + dot(erdy[0, rows, :], late, NT) + dot(erdy[1, rows, :], late, NT)).astype(bf16)
+        late = sl[b].astype(bf16)
+        d_c[rows, :] = (dot(ds[b], b_blk, TN) + dot(gy[0], late, NT) + dot(gy[1], late, NT)).astype(bf16)
         return carry
 
     lax.fori_loop(0, NB, step, 0)
@@ -281,9 +282,9 @@
     row, col = iota((N, N), 0), iota((N, N), 1)
     since = (row >= col).astype(f32)
     before = (row < col).astype(f32)
-    raw = dt[...] + bias[...]
+    raw = dt[...] + column(bias)
     sig = 1.0 / (1.0 + jnp.exp(-raw))
-    pull = jnp.exp(alog[...])
+    pull = jnp.exp(column(alog))
     ones = head_rows().astype(f32)
     for b in range(NB):
         at = lanes(b)
@@ -291,6 +292,8 @@
         d_rate = dot(row_own[:, at] - own[:, at] + row_carried[:, at], since, precision=HI) + past
         d_rate = d_rate + dot(carried[:, at], before, precision=HI)
         out[:, at] = (whole[:, at] - pull * d_rate) * sig[:, at]
+
+
 MESH = pl.DeviceIdType.MESH
 SHARD = 128
 HALF = HP // 2
@@ -301,24 +304,17 @@
     return lax.rem(value + size, size)
 
 
-def greet(seqs, heads):
+def greet(me, heads):
     barrier = pltpu.get_barrier_semaphore()
-    for s in seqs:
-        pl.semaphore_signal(barrier, inc=1, device_id={"seq": s}, device_id_type=MESH)
+
+    def step(k, carry):
+        pl.semaphore_signal(barrier, inc=1, device_id={"seq": lax.rem(me + k, SEQ)}, device_id_type=MESH)
+        return carry
+
+    lax.fori_loop(1, SEQ, step, 0)
     for h in heads:
         pl.semaphore_signal(barrier, inc=1, device_id={"head": h}, device_id_type=MESH)
-    pl.semaphore_wait(barrier, len(seqs) + len(heads))
-
-
-def greet_all(me):
-    barrier = pltpu.get_barrier_semaphore()
-
-    def step(k, carry):
-        pl.semaphore_signal(barrier, inc=1, device_id={"seq": lax.rem(me + k, SEQ)}, device_id_type=MESH)
-        return carry
-
-    lax.fori_loop(1, SEQ, step, 0)
-    pl.semaphore_wait(barrier, SEQ - 1)
+    pl.semaphore_wait(barrier, SEQ - 1 + len(heads))
 
 
 def remote(src, dst, ssem, rsem, **device):
@@ -410,11 +406,6 @@
         return self.at(z, mod(self.p + dp, 4), mod(self.q + dq, 4))
 
 
-def neighbours():
-    t = Torus(0)
-    return [t.place(dz=1), t.place(dp=1), t.place(dp=-1), t.place(dq=1), t.place(dq=-1)]
-
-
 class Gather:
     def __init__(self, half, buf, ssem, rsem):
         self.t, self.half, self.buf, self.ssem, self.rsem, self.n = Torus(half), half, buf, ssem, rsem, 0
@@ -470,9 +461,9 @@
             self.wait(shard)
             self.spread(shard)
 
-    def pass_on(self):
-        t = self.t
-        for k in range(4):
+    def pass_on(self, ks):
+        t = self.t
+        for k in ks:
             p = mod(t.p + (0, 1, 3, 2)[k], 4)
             for z, dq in ((0, -1), (1, 1)):
                 shard = t.at(z, p, mod(t.q + dq, 4))
@@ -643,52 +634,21 @@
 V = pltpu.VMEM
 DMA = pltpu.SemaphoreType.DMA
 
-
-def call(fn, outs, scratch, *args, cid=None):
-    return pl.pallas_call(
-        fn,
-        out_shape=[jax.ShapeDtypeStruct(s, d) for s, d in outs],
-        in_specs=[pl.BlockSpec(memory_space=pltpu.VMEM)] * len(args),
-        out_specs=[pl.BlockSpec(memory_space=pltpu.VMEM)] * len(outs),
-        scratch_shapes=scratch,
-        compiler_params=pltpu.CompilerParams(vmem_limit_bytes=60 << 20, collective_id=cid, has_side_effects=cid is not None),
-    )(*args)
-
-
-def k1(x, bm, cm, dt, bias, alog, keep_t, within, er, xw, sl, pd, step, r, step_t, r_t, st):
-    prepare(dt, bias, alog, step, r, step_t, r_t)
-    forward_local(x, bm, cm, r, r_t, step_t, keep_t, within, er, xw, sl, pd, st)
-
-
-def k2(x, cm, sl, pd, entering, er, skip, within, z, gain, y, sin, normed):
-    enter(x, cm, sl, pd, entering, er, skip, within, y, sin)
-    norm(y, z, gain, normed)
-
-
-def k3(y, within, x, z, gain, skip, d_normed, cm, r_t, keep_t, er, d_z, d_y, row_own, row_carried, erdy, gl, qd, gt, work, carried):
-    unnorm(y, within, x, z, gain, skip, d_normed, d_z, d_y, work, carried)
-    gather_heads(work, row_own)
-    gather_heads(carried, row_carried)
-    state_grad(cm, r_t, keep_t, er, d_y, erdy, gl, qd, gt)
-
-
-def k4(x, bm, cm, r, r_t, step_t, skip, d_y0, xw, erdy, sin, gl, qd, arriving,
-       dt, bias, alog, step, row_own, row_carried, d_x, d_b, d_c, out, d_y, v, ds, ge, psi, own, s1, s2, s3):
-    d_y[...] = d_y0[...]
-    backward_within(x, bm, cm, r, r_t, step_t, d_y, v, ds)
-    backward_rest(x, bm, cm, r_t, step_t, skip, d_y, v, ds, xw, erdy, sin, gl, qd, arriving, ge, psi, own, d_x, d_b, d_c)
-    gather_heads(own, s1)
-    gather_heads(v, s2)
-    gather_heads(d_y, s3)
-    steps_grad(dt, bias, alog, step, psi, row_own, row_carried, s1, s2, s3, out)
-
-
-def kx(backward, state, decay, result, *bufs):
-    me = lax.axis_index("seq")
-    greet_all(me)
-    exchange_out(me, state, decay, *bufs[:4])
-    exchange_fold(me, backward, *bufs)
-    exchange_in(me, result, *bufs)
+SCRATCH = {
+    "step": V((H, T), f32), "r": V((H, T), f32), "step_t": V((T, H), f32), "r_t": V((T, H), f32),
+    "keep_t": V((NB, 1, H), f32), "skips": V((1, HP), f32),
+    "within": V((T, HP), f32), "er": V((T, HP), f32), "xw": V((T, HP), bf16),
+    "sl": V((NB + 1, N, HP), f32), "pd": V((NB + 1, 1, HP), f32), "st": V((N, HP), f32),
+    "y": V((T, HP), f32), "normed": V((T, HP), bf16), "dn": V((T, HP), f32), "d_y": V((T, HP), f32),
+    "row_own": V((H, T), f32), "row_carried": V((H, T), f32), "s1": V((H, T), f32), "s2": V((H, T), f32), "s3": V((H, T), f32),
+    "gl": V((NB, N, HP), f32), "qd": V((NB, 1, HP), f32),
+    "entering": V((N, HP), f32),
+    "ds": V((NB, N, N), bf16), "ge": V((2, N, HP), bf16), "gy": V((2, N, HP), bf16), "psi": V((NB, 8, HP), f32),
+    "wbuf": V((2, SEQ, SHARD, HALF), bf16), "cbuf": V((4, T, HP), bf16),
+    "ws": DMA((2, 31)), "wr": DMA((2, SEQ)), "cs": DMA((6,)), "cr": DMA((4, 2)), "local": DMA((3,)),
+    "out": V((2, SLOTS, SHARD, HALF), bf16), "inn": V((2, SLOTS, SHARD, HALF), bf16),
+    "ss": DMA((2, SLOTS)), "rs": DMA((2, SLOTS)), "acc": V((2, 2, 4, SHARD, HALF), f32),
+}
 
 
 def multiply(cots, ws, out):
@@ -706,72 +666,115 @@
     lax.fori_loop(0, 4, step, 0)
 
 
-def kg(w, cot, d_normed, cots, wbuf, cbuf, ws, wr, cs, cr):
-    heads = Heads(cbuf, cs, cr)
-    gathers = [Gather(h, wbuf, ws, wr) for h in (0, 1)]
+def kernel(x, z, bm, cm, dt, bias, alog, skip, gain, resets, w, cot, d_x, d_z, d_b, d_c, d_dt, d_w, *refs):
+    count = len(SCRATCH)
+    s = dict(zip(SCRATCH, refs[:count]))
+    swap = refs[count:]
     me = lax.axis_index("seq")
-    wbuf[0, me] = w[:, :HALF]
-    wbuf[1, me] = w[:, HALF:]
-    cbuf[heads.h] = cot[...]
-    greet(neighbours(), [heads.core, heads.chip])
-    for name in ("own", "across", "near", "far", "pass_on", "rest"):
-        for g in gathers:
-            getattr(g, name)()
-        if name in ("own", "across", "rest"):
-            getattr(heads, name)()
-    multiply(cbuf, wbuf, d_normed)
-    cots[...] = cbuf[...]
-    for g in gathers:
-        g.close()
-    heads.close()
-
-
-def ks(cots, normed, result, out, inn, ss, rs, acc):
+    step, r, step_t, r_t, keep_t, skips = (s[k] for k in ("step", "r", "step_t", "r_t", "keep_t", "skips"))
+    within, er, xw, sl, pd, st, y = (s[k] for k in ("within", "er", "xw", "sl", "pd", "st", "y"))
+    normed, dn, d_y, gl, qd = (s[k] for k in ("normed", "dn", "d_y", "gl", "qd"))
+    entering, cbuf, wbuf, gt = s["entering"], s["cbuf"], s["wbuf"], st
+
+    heads = Heads(cbuf, s["cs"], s["cr"])
+    gathers = [Gather(h, wbuf, s["ws"], s["wr"]) for h in (0, 1)]
+
     def part(half, shard):
         block, at = lax.div(shard, 8), lax.rem(shard, 8)
         cols = pl.ds(pl.multiple_of(at * SHARD, SHARD), SHARD)
-        return dot(cots[block, :, cols], normed[:, HALF * half : HALF * (half + 1)], TN)
-
-    greet(neighbours(), [])
-    scatters = [Scatter(h, part, out, inn, ss, rs, acc, result) for h in (0, 1)]
-    for name in ("q_far", "q_near", "q_pass", "q_own", "p_far", "p_near", "p_own", "z_out", "z_in", "close"):
-        for s in scatters:
-            getattr(s, name)()
+        return dot(cbuf[block, :, cols], normed[:, HALF * half : HALF * (half + 1)], TN)
+
+    scatters = [Scatter(h, part, s["out"], s["inn"], s["ss"], s["rs"], s["acc"], d_w) for h in (0, 1)]
+
+    def gather(name, *args):
+        for g in gathers:
+            getattr(g, name)(*args)
+
+    def scatter(*names):
+        for name in names:
+            for g in scatters:
+                getattr(g, name)()
+
+    def block(b):
+        forward_block(b, x, bm, cm, r, r_t, step_t, keep_t, within, er, xw, sl, pd, st)
+
+    local = s["local"]
+    mine = [pltpu.make_async_copy(w.at[:, pl.ds(HALF * h, HALF)], wbuf.at[h, me], local.at[h]) for h in (0, 1)]
+    mine.append(pltpu.make_async_copy(cot, cbuf.at[heads.h], local.at[2]))
+    for copy in mine:
+        copy.start()
+    for copy in mine:
+        copy.wait()
+    greet(me, [heads.core, heads.chip])
+
+    gather("own")
+    heads.own()
+    prepare(dt, bias, alog, resets, skip, step, r, step_t, r_t, keep_t, skips)
+    forward_start(pd, st)
+    block(0)
+    gather("across")
+    block(1)
+    gather("near")
+    block(2)
+    gather("far")
+    block(3)
+    sl[NB] = st[...]
+    exchange_out(me, st, pd[NB], *swap[:4])
+    gather("pass_on", (0,))
+    heads.across()
+    exchange_fold(me, False, *swap)
+    gather("pass_on", (1,))
+    exchange_in(me, entering, *swap)
+    enter(x, cm, sl, pd, entering, er, skips, within, y)
+    gather("pass_on", (2,))
+    norm(y, z, gain, normed)
+    gather("pass_on", (3,))
+    heads.rest()
+    scatter("q_far")
+    gather("rest")
+    scatter("q_near")
+    multiply(cbuf, wbuf, dn)
+    scatter("q_pass")
+    unnorm(y, within, x, z, gain, skips, dn, d_z, d_y)
+    scatter("q_own")
+    gather_heads(y, s["row_own"])
+    gather_heads(dn, s["row_carried"])
+    state_grad(cm, r_t, keep_t, er, d_y, gl, qd, gt)
+    exchange_out(me, gt, pd[NB], *swap[:4])
+    scatter("p_far")
+    backward_within(x, bm, cm, r, r_t, step_t, d_y, dn, s["ds"])
+    exchange_fold(me, True, *swap)
+    scatter("p_near", "p_own", "z_out")
+    exchange_in(me, entering, *swap)
+    backward_rest(x, bm, cm, r_t, step_t, skips, d_y, dn, s["ds"], xw, er, sl, gl, qd, entering, s["ge"], s["gy"], s["psi"], y, d_x, d_b, d_c)
+    gather_heads(y, s["s1"])
+    gather_heads(dn, s["s2"])
+    gather_heads(d_y, s["s3"])
+    steps_grad(dt, bias, alog, step, s["psi"], s["row_own"], s["row_carried"], s["s1"], s["s2"], s["s3"], d_dt)
+    scatter("z_in", "close")
+    gather("close")
+    heads.close()
 
 
 def body(x, z, bm, cm, dt, bias, alog, skip, gain, resets, w, cot):
-    keep = 1.0 - resets.astype(f32)
-    keep_t = keep.T[:, None, :]
-    skip = jnp.repeat(skip, 64)[None]
-    gain = gain[None]
-    bias, alog = bias[:, None], alog[:, None]
-    F, B = f32, bf16
-    within, er, xw, sl, pd, step, r, step_t, r_t = call(
-        k1, [((T, HP), F), ((T, HP), F), ((T, HP), B), ((NB + 1, N, HP), F), ((NB + 1, 1, HP), F), ((H, T), F), ((H, T), F), ((T, H), F), ((T, H), F)],
-        [V((N, HP), F)], x, bm, cm, dt, bias, alog, keep_t)
-    entering = call(functools.partial(kx, False), [((N, HP), F)], EXCHANGE, sl[NB], pd[NB], cid=0)[0]
-    y, sin, normed = call(k2, [((T, HP), F), ((NB, N, HP), F), ((T, HP), B)], [], x, cm, sl, pd, entering, er, skip, within, z, gain)
-    d_normed, cots = call(
-        kg, [((T, HP), F), ((4, T, HP), B)],
-        [V((2, SEQ, SHARD, HALF), B), V((4, T, HP), B), DMA((2, 31)), DMA((2, SEQ)), DMA((6,)), DMA((4, 2))], w, cot, cid=2)
-    d_z, d_y, row_own, row_carried, erdy, gl, qd, gt = call(
-        k3, [((T, HP), B), ((T, HP), F), ((H, T), F), ((H, T), F), ((2, T, HP), B), ((NB, N, HP), F), ((NB + 1, 1, HP), F), ((N, HP), F)],
-        [V((T, HP), F), V((T, HP), F)], y, within, x, z, gain, skip, d_normed, cm, r_t, keep_t, er)
-    arriving = call(functools.partial(kx, True), [((N, HP), F)], EXCHANGE, gt, pd[NB], cid=1)[0]
-    d_x, d_b, d_c, out = call(
-        k4, [((T, HP), B), ((T, N), B), ((T, N), B), ((H, T), F)],
-        [V((T, HP), F), V((T, HP), F), V((NB, N, N), B), V((2, N, HP), B), V((NB, 8, HP), F), V((T, HP), F), V((H, T), F), V((H, T), F), V((H, T), F)],
-        x, bm, cm, r, r_t, step_t, skip, d_y, xw, erdy, sin, gl, qd, arriving, dt, bias, alog, step, row_own, row_carried)
-    d_w = call(
-        ks, [((SHARD, HP), F)],
-        [V((2, SLOTS, SHARD, HALF), B), V((2, SLOTS, SHARD, HALF), B), DMA((2, SLOTS)), DMA((2, SLOTS)), V((2, 2, 4, SHARD, HALF), F)],
-        cots, normed, cid=3)[0]
-    return d_x, d_z, d_b, d_c, out, d_w
+    outs = [((T, HP), bf16), ((T, HP), bf16), ((T, N), bf16), ((T, N), bf16), ((H, T), f32), ((SHARD, HP), f32)]
+    vmem = pl.BlockSpec(memory_space=pltpu.VMEM)
+    return pl.pallas_call(
+        kernel,
+        out_shape=[jax.ShapeDtypeStruct(shape, kind) for shape, kind in outs],
+        in_specs=[vmem] * 10 + [pl.BlockSpec(memory_space=pl.ANY)] * 2,
+        out_specs=[vmem] * len(outs),
+        scratch_shapes=list(SCRATCH.values()) + EXCHANGE,
+        compiler_params=pltpu.CompilerParams(vmem_limit_bytes=63 << 20, collective_id=0, has_side_effects=True),
+    )(x, z, bm, cm, dt, bias[None], alog[None], skip[None], gain[None], resets, w, cot)
 
 
 def solution(mesh):
     s, h = P("seq", "head"), P("head")
     return jax.shard_map(
-        body, mesh=mesh,
+        body,
+        mesh=mesh,
         in_specs=(s, s, s, s, P("head", "seq"), h, h, h, h, P("head", "seq"), s, s),
-        out_specs=(s, s, s, s, P("head", "seq"), s), check_vma=False)
+        out_specs=(s, s, s, s, P("head", "seq"), s),
+        check_vma=False,
+    )

time: 253 us -> 152 us (0.60)
  Pallas kernels: 242 us -> 144 us
    pallas_call x8 -> x1, Pallas kernels: 242 us -> 144 us  [body(): pl.pallas_call(kernel, out_shape=[jax.ShapeDtypeStruct(shape, kind) for s...]
    unnamed x3 -> x19, local copies, waits for them, and re-layouts: 0.8 us -> 7.43 us
    broadcast_in_dim x3 -> x0, local copies, waits for them, and re-layouts: 3.37 us -> none  [the longest x2 2.65 us: body(): bias, alog = (bias[:, None], alog[:, None])]
    squeeze x2 -> x0, local copies, waits for them, and re-layouts: 3.16 us -> none  [the longest x1 1.88 us: body(): sl[NB]]
where the time goes in v2:
time: 152 us
  Pallas kernels  144 us (95%)
  local copies, waits for them, and re-layouts  7.43 us (5%)
    pallas_call x1, Pallas kernels, body(): pl.pallas_call(kernel, out_shape=[jax.ShapeDtypeStruct(shape, kind) for s...  144 us
    unnamed x19, local copies, waits for them, and re-layouts  7.43 us

profile of v2, /device:TPU:0, one launch (start us, length us, event | category | flops | bytes accessed | tf_op | source)
XLA Modules:
  0.0 151.7 jit_solution(1413904216180498295)
XLA Ops:
  0.6 0.0 copy-start.5
  0.6 0.7 copy-done.5
  1.3 0.7 copy.18.resets
  2.0 143.6 %shard_map.163 = (bf16[512,1024]{1,0:T(8,128)(2,1)}, bf16[512,1024]{1,0:T(8,128)(2,1)}, bf16[512,128]{1,0:T(8,128)(2,1)}, bf16[512,128]{1,0:T(8,128)(2,1)}, f32[16,512]{1,0:T(8,128)}, /*index=5*/f32[128,1024]{1,0:T(8,128)}) custom-call(bf16[512,1024]{1,0:T(8,128)(2,1)} %x.1, bf16[512,1024]{1,0:T(8,128)(2,1)} %z.1, bf16[512,128]{1,0:T(8,128)(2,1)} %bm.1, ...), custom_call_target="tpu_custom_call" | custom-call | tf_op jit(solution)/shard_map/pallas_call | solution.py:762
  145.6 0.0 copy-start
  145.6 2.4 %copy.25 = bf16[512,1024]{1,0:T(8,128)(2,1)} copy(bf16[512,1024]{1,0:T(8,128)(2,1)} %get-tuple-element.12) | data formatting | bytes 2097152
  148.0 0.0 copy-done
  148.0 0.0 copy-start.3
  148.0 0.0 copy-start.2
  148.0 0.0 copy-start.4
  148.0 1.0 copy.26
  149.0 0.0 copy-done.3
  149.0 0.0 copy-start.1
  149.0 0.7 copy.27
  149.6 0.0 copy-done.2
  149.6 0.7 copy.28
  150.3 0.0 copy-done.4
  150.3 0.6 copy.29
  150.9 0.0 copy-done.1
  150.9 0.8 copy.30
Async XLA Ops:
  0.6 0.7 copy-start.5
  145.6 2.4 %copy-start = (bf16[512,1024]{1,0:T(8,128)(2,1)S(1)}, bf16[512,1024]{1,0:T(8,128)(2,1)}, u32[]{:S(2)}) copy-start(bf16[512,1024]{1,0:T(8,128)(2,1)} %get-tuple-element.13) | copy-start | bytes 3145732
  148.0 1.0 copy-start.3
  148.0 1.7 %copy-start.2 = (bf16[512,128]{1,0:T(8,128)(2,1)S(1)}, bf16[512,128]{1,0:T(8,128)(2,1)}, u32[]{:S(2)}) copy-start(bf16[512,128]{1,0:T(8,128)(2,1)} %get-tuple-element.15) | copy-start | bytes 393220
  148.0 2.3 %copy-start.4 = (f32[16,512]{1,0:T(8,128)S(1)}, f32[16,512]{1,0:T(8,128)}, u32[]{:S(2)}) copy-start(f32[16,512]{1,0:T(8,128)} %get-tuple-element.16) | copy-start | bytes 98308
  149.0 1.9 %copy-start.1 = (f32[128,1024]{1,0:T(8,128)S(1)}, f32[128,1024]{1,0:T(8,128)}, u32[]{:S(2)}) copy-start(f32[128,1024]{1,0:T(8,128)} %get-tuple-element.17) | copy-start | bytes 1572868

commit v3 on v2

--- a/solution.py
+++ b/solution.py
@@ -244,7 +244,7 @@
     lax.fori_loop(0, NB, step, 0)
 
 
-def backward_rest(x, bm, cm, r_t, step_t, skip, d_y, v, ds, xw, er, sl, gl, qd, arriving, ge, gy, psi, own, d_x, d_b, d_c):
+def backward_rest(span, x, bm, cm, r_t, step_t, skip, d_y, v, ds, xw, er, sl, gl, qd, arriving, ge, gy, psi, own, d_x, d_b, d_c):
     def step(b, carry):
         base = pl.multiple_of(b * N, N)
         rows = pl.ds(base, N)
@@ -275,7 +275,7 @@
         d_c[rows, :] = (dot(ds[b], b_blk, TN) + dot(gy[0], late, NT) + dot(gy[1], late, NT)).astype(bf16)
         return carry
 
-    lax.fori_loop(0, NB, step, 0)
+    lax.fori_loop(*span, step, 0)
 
 
 def steps_grad(dt, bias, alog, step, psi, row_own, row_carried, own, carried, whole, out):
@@ -334,26 +334,29 @@
     lax.fori_loop(1, SEQ, step, 0)
 
 
-def to_copy(me, buf, land, ssem, rsem, other):
-    return remote(buf.at[other], land.at[me], ssem.at[other], rsem.at[me], seq=other)
-
-
-def from_copy(me, buf, land, ssem, rsem, other):
-    return remote(buf.at[me], land.at[other], ssem.at[me], rsem.at[other], seq=other)
+def to_copy(me, rows, buf, land, ssem, rsem, other):
+    return remote(buf.at[other, :rows], land.at[me, :rows], ssem.at[other], rsem.at[me], seq=other)
+
+
+def from_copy(me, rows, buf, land, ssem, rsem, other):
+    return remote(buf.at[me, :rows], land.at[other, :rows], ssem.at[me], rsem.at[other], seq=other)
 
 
 def exchange_out(me, state, decay, out1, in1, s1, r1):
+    rows = SLICE if decay is None else SLICE + 8
     for j in range(NP):
         for i in range(N // SLICE):
             k = j * (N // SLICE) + i
             out1[k, :SLICE] = state[SLICE * i : SLICE * (i + 1), lanes(j)]
-            out1[k, SLICE:] = jnp.broadcast_to(decay[:, lanes(j)], (8, N))
-    each_other(me, lambda o: to_copy(me, out1, in1, s1, r1, o).start())
-    in1[me] = out1[me]
+            if decay is not None:
+                out1[k, SLICE:] = jnp.broadcast_to(decay[:, lanes(j)], (8, N))
+    each_other(me, lambda o: to_copy(me, rows, out1, in1, s1, r1, o).start())
+    in1[me, :rows] = out1[me, :rows]
 
 
 def exchange_fold(me, backward, out1, in1, s1, r1, out2, in2, s2, r2):
-    each_other(me, lambda o: from_copy(me, out1, in1, s1, r1, o).wait_recv())
+    rows = SLICE if backward else SLICE + 8
+    each_other(me, lambda o: from_copy(me, rows, out1, in1, s1, r1, o).wait_recv())
 
     def step(i, total):
         at = SEQ - 1 - i if backward else i
@@ -361,19 +364,20 @@
         return total * in1[at, SLICE : SLICE + 1] + in1[at, :SLICE]
 
     lax.fori_loop(0, SEQ, step, jnp.zeros((SLICE, N), f32))
-    each_other(me, lambda o: to_copy(me, out2, in2, s2, r2, o).start())
+    each_other(me, lambda o: to_copy(me, SLICE, out2, in2, s2, r2, o).start())
     in2[me] = out2[me]
 
 
-def exchange_in(me, result, out1, in1, s1, r1, out2, in2, s2, r2):
-    each_other(me, lambda o: from_copy(me, out2, in2, s2, r2, o).wait_recv())
+def exchange_in(me, backward, result, out1, in1, s1, r1, out2, in2, s2, r2):
+    rows = SLICE if backward else SLICE + 8
+    each_other(me, lambda o: from_copy(me, SLICE, out2, in2, s2, r2, o).wait_recv())
     for j in range(NP):
         for i in range(N // SLICE):
             result[SLICE * i : SLICE * (i + 1), lanes(j)] = in2[j * (N // SLICE) + i]
 
     def done(o):
-        to_copy(me, out1, in1, s1, r1, o).wait_send()
-        to_copy(me, out2, in2, s2, r2, o).wait_send()
+        to_copy(me, rows, out1, in1, s1, r1, o).wait_send()
+        to_copy(me, SLICE, out2, in2, s2, r2, o).wait_send()
 
     each_other(me, done)
 
@@ -470,11 +474,26 @@
                 self.wait(shard)
                 self.send(shard, t.place(dq=-dq))
 
-    def rest(self):
+    def rest(self, ends):
         t = self.t
         for p in range(4):
-            for z, dq in ((1, -1), (0, 1), (0, 2), (1, 2)):
+            for z, dq in ends:
                 self.wait(t.at(z, p, mod(t.q + dq, 4)))
+
+    def multiply(self, cots, out, dqs, first):
+        t = self.t
+        at = slice(HALF * self.half, HALF * (self.half + 1))
+        total = None if first else out[:, at]
+        for dq in dqs:
+            for p in range(4):
+                pair = [t.at(z, p, mod(t.q + dq, 4)) for z in (0, 1)]
+                left = [
+                    cots[lax.div(k, 8), :, pl.ds(pl.multiple_of(lax.rem(k, 8) * SHARD, SHARD), SHARD)] for k in pair
+                ]
+                right = [self.buf[self.half, k] for k in pair]
+                term = dot(jnp.concatenate(left, axis=1), jnp.concatenate(right, axis=0))
+                total = term if total is None else total + term
+        out[:, at] = total
 
     def close(self):
         for copy in self.sent:
@@ -542,8 +561,8 @@
         return self.inn[self.half, slot].astype(f32)
 
     def loop(self, fn):
-        def step(p, carry):
-            fn(p)
+        def step(i, carry):
+            fn(lax.rem(self.t.p + 2 + 3 * i + 3 * lax.div(i * (i - 1), 2), 4))
             return carry
 
         lax.fori_loop(0, 4, step, 0)
@@ -651,21 +670,6 @@
 }
 
 
-def multiply(cots, ws, out):
-    def step(i, carry):
-        half, tile = lax.div(i, 2), lax.rem(i, 2)
-        at = pl.ds(pl.multiple_of(tile * 256, 256), 256)
-        total = None
-        for k in range(4):
-            rows = ws[half, 8 * k : 8 * k + 8, :, at].reshape(1024, 256)
-            term = dot(cots[k], rows)
-            total = term if total is None else total + term
-        out[:, pl.ds(pl.multiple_of(i * 256, 256), 256)] = total
-        return carry
-
-    lax.fori_loop(0, 4, step, 0)
-
-
 def kernel(x, z, bm, cm, dt, bias, alog, skip, gain, resets, w, cot, d_x, d_z, d_b, d_c, d_dt, d_w, *refs):
     count = len(SCRATCH)
     s = dict(zip(SCRATCH, refs[:count]))
@@ -703,9 +707,9 @@
     mine.append(pltpu.make_async_copy(cot, cbuf.at[heads.h], local.at[2]))
     for copy in mine:
         copy.start()
+    greet(me, [heads.core, heads.chip])
     for copy in mine:
         copy.wait()
-    greet(me, [heads.core, heads.chip])
 
     gather("own")
     heads.own()
@@ -722,31 +726,37 @@
     exchange_out(me, st, pd[NB], *swap[:4])
     gather("pass_on", (0,))
     heads.across()
+    gather("pass_on", (1,))
     exchange_fold(me, False, *swap)
-    gather("pass_on", (1,))
-    exchange_in(me, entering, *swap)
+    gather("pass_on", (2,))
+    heads.rest()
+    gather("multiply", cbuf, dn, (0,), True)
+    exchange_in(me, False, entering, *swap)
+    gather("pass_on", (3,))
     enter(x, cm, sl, pd, entering, er, skips, within, y)
-    gather("pass_on", (2,))
     norm(y, z, gain, normed)
-    gather("pass_on", (3,))
-    heads.rest()
     scatter("q_far")
-    gather("rest")
+    gather("rest", ((1, -1), (0, 1)))
+    gather("multiply", cbuf, dn, (1, 3), False)
     scatter("q_near")
-    multiply(cbuf, wbuf, dn)
+    gather("rest", ((0, 2), (1, 2)))
+    gather("multiply", cbuf, dn, (2,), False)
+    unnorm(y, within, x, z, gain, skips, dn, d_z, d_y)
+    state_grad(cm, r_t, keep_t, er, d_y, gl, qd, gt)
+    exchange_out(me, gt, None, *swap[:4])
     scatter("q_pass")
-    unnorm(y, within, x, z, gain, skips, dn, d_z, d_y)
+    gather_heads(dn, s["row_carried"])
     scatter("q_own")
-    gather_heads(y, s["row_own"])
-    gather_heads(dn, s["row_carried"])
-    state_grad(cm, r_t, keep_t, er, d_y, gl, qd, gt)
-    exchange_out(me, gt, pd[NB], *swap[:4])
-    scatter("p_far")
     backward_within(x, bm, cm, r, r_t, step_t, d_y, dn, s["ds"])
     exchange_fold(me, True, *swap)
-    scatter("p_near", "p_own", "z_out")
-    exchange_in(me, entering, *swap)
-    backward_rest(x, bm, cm, r_t, step_t, skips, d_y, dn, s["ds"], xw, er, sl, gl, qd, entering, s["ge"], s["gy"], s["psi"], y, d_x, d_b, d_c)
+    scatter("p_far")
+    gather_heads(y, s["row_own"])
+    scatter("p_near")
+    exchange_in(me, True, entering, *swap)
+    late = (x, bm, cm, r_t, step_t, skips, d_y, dn, s["ds"], xw, er, sl, gl, qd, entering, s["ge"], s["gy"], s["psi"], y, d_x, d_b, d_c)
+    backward_rest((0, 2), *late)
+    scatter("p_own", "z_out")
+    backward_rest((2, 4), *late)
     gather_heads(y, s["s1"])
     gather_heads(dn, s["s2"])
     gather_heads(d_y, s["s3"])
@@ -756,10 +766,16 @@
     heads.close()
 
 
+def finish(*refs):
+    half = len(refs) // 2
+    for source, target in zip(refs[:half], refs[half:]):
+        target[...] = source[...]
+
+
 def body(x, z, bm, cm, dt, bias, alog, skip, gain, resets, w, cot):
     outs = [((T, HP), bf16), ((T, HP), bf16), ((T, N), bf16), ((T, N), bf16), ((H, T), f32), ((SHARD, HP), f32)]
     vmem = pl.BlockSpec(memory_space=pltpu.VMEM)
-    return pl.pallas_call(
+    results = pl.pallas_call(
         kernel,
         out_shape=[jax.ShapeDtypeStruct(shape, kind) for shape, kind in outs],
         in_specs=[vmem] * 10 + [pl.BlockSpec(memory_space=pl.ANY)] * 2,
@@ -767,6 +783,15 @@
         scratch_shapes=list(SCRATCH.values()) + EXCHANGE,
         compiler_params=pltpu.CompilerParams(vmem_limit_bytes=63 << 20, collective_id=0, has_side_effects=True),
     )(x, z, bm, cm, dt, bias[None], alog[None], skip[None], gain[None], resets, w, cot)
+    blocks = [pl.BlockSpec((shape[0] // 4, shape[1]), lambda i: (i, 0)) for shape, kind in outs]
+    blocks[4] = pl.BlockSpec((H, T // 4), lambda i: (0, i))
+    return pl.pallas_call(
+        finish,
+        grid=(4,),
+        out_shape=[jax.ShapeDtypeStruct(shape, kind) for shape, kind in outs],
+        in_specs=blocks,
+        out_specs=blocks,
+    )(*results)
 
 
 def solution(mesh):

time: 152 us -> 146 us (0.961)
  local copies, waits for them, and re-layouts: 7.43 us -> 1.35 us
    unnamed x19 -> x3, local copies, waits for them, and re-layouts: 7.43 us -> 1.35 us
    pallas_call x0 -> x1, Pallas kernels: none -> 4.1 us  [body(): pl.pallas_call(finish, grid=(4,), out_shape=[jax.ShapeDtypeStruct(shape,...]
    pallas_call x1, Pallas kernels: 144 us -> 140 us  [body(): pl.pallas_call(kernel, out_shape=[jax.ShapeDtypeStruct(shape, kind) for s...]
where the time goes in v3:
time: 146 us
  Pallas kernels  144 us (99%)
    pallas_call x1, Pallas kernels, body(): pl.pallas_call(kernel, out_shape=[jax.ShapeDtypeStruct(shape, kind) for s...  140 us
    pallas_call x1, Pallas kernels, body(): pl.pallas_call(finish, grid=(4,), out_shape=[jax.ShapeDtypeStruct(shape,...  4.1 us

profile of v3, /device:TPU:0, one launch (start us, length us, event | category | flops | bytes accessed | tf_op | source)
XLA Modules:
  0.0 146.1 jit_solution(798717812967638827)
XLA Ops:
  0.6 0.0 copy-start
  0.6 0.7 copy-done
  1.3 0.7 copy.18.resets
  2.0 139.8 %shard_map.163 = (bf16[512,1024]{1,0:T(8,128)(2,1)}, bf16[512,1024]{1,0:T(8,128)(2,1)}, bf16[512,128]{1,0:T(8,128)(2,1)}, bf16[512,128]{1,0:T(8,128)(2,1)}, f32[16,512]{1,0:T(8,128)}, /*index=5*/f32[128,1024]{1,0:T(8,128)}) custom-call(bf16[512,1024]{1,0:T(8,128)(2,1)} %x.1, bf16[512,1024]{1,0:T(8,128)(2,1)} %z.1, bf16[512,128]{1,0:T(8,128)(2,1)} %bm.1, ...), custom_call_target="tpu_custom_call" | custom-call | tf_op jit(solution)/shard_map/pallas_call | solution.py:778
  141.8 4.1 %shard_map.164 = (bf16[512,1024]{1,0:T(8,128)(2,1)}, bf16[512,1024]{1,0:T(8,128)(2,1)}, bf16[512,128]{1,0:T(8,128)(2,1)}, bf16[512,128]{1,0:T(8,128)(2,1)}, f32[16,512]{1,0:T(8,128)}, /*index=5*/f32[128,1024]{1,0:T(8,128)}) custom-call(bf16[512,1024]{1,0:T(8,128)(2,1)} %get-tuple-element.12.refs_0_, bf16[512,1024]{1,0:T(8,128)(2,1)} %get-tuple-element.13.refs_1_, ...), custom_call_target="tpu_custom_call" | custom-call | tf_op jit(solution)/shard_map/pallas_call | solution.py:788
Async XLA Ops:
  0.6 0.7 copy-start

commit v4 on v3

--- a/solution.py
+++ b/solution.py
@@ -720,19 +720,19 @@
     block(1)
     gather("near")
     block(2)
-    gather("far")
     block(3)
     sl[NB] = st[...]
     exchange_out(me, st, pd[NB], *swap[:4])
+    gather("far")
     gather("pass_on", (0,))
     heads.across()
+    exchange_fold(me, False, *swap)
     gather("pass_on", (1,))
-    exchange_fold(me, False, *swap)
     gather("pass_on", (2,))
     heads.rest()
     gather("multiply", cbuf, dn, (0,), True)
+    gather("pass_on", (3,))
     exchange_in(me, False, entering, *swap)
-    gather("pass_on", (3,))
     enter(x, cm, sl, pd, entering, er, skips, within, y)
     norm(y, z, gain, normed)
     scatter("q_far")

time: 146 us -> 143 us (0.979)
  Pallas kernels: 144 us -> 140 us
    pallas_call x1, Pallas kernels: 140 us -> 136 us  [body(): pl.pallas_call(kernel, out_shape=[jax.ShapeDtypeStruct(shape, kind) for s...]
where the time goes in v4:
time: 143 us
  Pallas kernels  140 us (98%)
    pallas_call x1, Pallas kernels, body(): pl.pallas_call(kernel, out_shape=[jax.ShapeDtypeStruct(shape, kind) for s...  136 us
    pallas_call x1, Pallas kernels, body(): pl.pallas_call(finish, grid=(4,), out_shape=[jax.ShapeDtypeStruct(shape,...  4.1 us

profile of v4, /device:TPU:0, one launch (start us, length us, event | category | flops | bytes accessed | tf_op | source)
XLA Modules:
  0.0 142.6 jit_solution(10951552801161335415)
XLA Ops:
  0.6 0.0 copy-start
  0.6 0.7 copy-done
  1.3 0.7 copy.18.resets
  2.0 136.3 %shard_map.163 = (bf16[512,1024]{1,0:T(8,128)(2,1)}, bf16[512,1024]{1,0:T(8,128)(2,1)}, bf16[512,128]{1,0:T(8,128)(2,1)}, bf16[512,128]{1,0:T(8,128)(2,1)}, f32[16,512]{1,0:T(8,128)}, /*index=5*/f32[128,1024]{1,0:T(8,128)}) custom-call(bf16[512,1024]{1,0:T(8,128)(2,1)} %x.1, bf16[512,1024]{1,0:T(8,128)(2,1)} %z.1, bf16[512,128]{1,0:T(8,128)(2,1)} %bm.1, ...), custom_call_target="tpu_custom_call" | custom-call | tf_op jit(solution)/shard_map/pallas_call | solution.py:778
  138.3 4.1 %shard_map.164 = (bf16[512,1024]{1,0:T(8,128)(2,1)}, bf16[512,1024]{1,0:T(8,128)(2,1)}, bf16[512,128]{1,0:T(8,128)(2,1)}, bf16[512,128]{1,0:T(8,128)(2,1)}, f32[16,512]{1,0:T(8,128)}, /*index=5*/f32[128,1024]{1,0:T(8,128)}) custom-call(bf16[512,1024]{1,0:T(8,128)(2,1)} %get-tuple-element.12.refs_0_, bf16[512,1024]{1,0:T(8,128)(2,1)} %get-tuple-element.13.refs_1_, ...), custom_call_target="tpu_custom_call" | custom-call | tf_op jit(solution)/shard_map/pallas_call | solution.py:788
Async XLA Ops:
  0.6 0.7 copy-start

commit v5 on v4

--- a/solution.py
+++ b/solution.py
@@ -343,7 +343,7 @@
 
 
 def exchange_out(me, state, decay, out1, in1, s1, r1):
-    rows = SLICE if decay is None else SLICE + 8
+    rows = SLICE if decay is None else SLICE + 1
     for j in range(NP):
         for i in range(N // SLICE):
             k = j * (N // SLICE) + i
@@ -355,7 +355,7 @@
 
 
 def exchange_fold(me, backward, out1, in1, s1, r1, out2, in2, s2, r2):
-    rows = SLICE if backward else SLICE + 8
+    rows = SLICE if backward else SLICE + 1
     each_other(me, lambda o: from_copy(me, rows, out1, in1, s1, r1, o).wait_recv())
 
     def step(i, total):
@@ -369,7 +369,7 @@
 
 
 def exchange_in(me, backward, result, out1, in1, s1, r1, out2, in2, s2, r2):
-    rows = SLICE if backward else SLICE + 8
+    rows = SLICE if backward else SLICE + 1
     each_other(me, lambda o: from_copy(me, SLICE, out2, in2, s2, r2, o).wait_recv())
     for j in range(NP):
         for i in range(N // SLICE):

time: 143 us -> 142 us (level)
  no operation moved by 1% of the time
where the time goes in v5:
time: 142 us; the launch traced here: 141 us
  Pallas kernels  139 us (98%)
    pallas_call x1, Pallas kernels, body(): pl.pallas_call(kernel, out_shape=[jax.ShapeDtypeStruct(shape, kind) for s...  135 us
    pallas_call x1, Pallas kernels, body(): pl.pallas_call(finish, grid=(4,), out_shape=[jax.ShapeDtypeStruct(shape,...  4.1 us

profile of v5, /device:TPU:0, one launch (start us, length us, event | category | flops | bytes accessed | tf_op | source)
XLA Modules:
  0.0 141.3 jit_solution(2121573096576189638)
XLA Ops:
  0.6 0.0 copy-start
  0.6 0.7 copy-done
  1.3 0.7 copy.18.resets
  2.0 135.1 %shard_map.163 = (bf16[512,1024]{1,0:T(8,128)(2,1)}, bf16[512,1024]{1,0:T(8,128)(2,1)}, bf16[512,128]{1,0:T(8,128)(2,1)}, bf16[512,128]{1,0:T(8,128)(2,1)}, f32[16,512]{1,0:T(8,128)}, /*index=5*/f32[128,1024]{1,0:T(8,128)}) custom-call(bf16[512,1024]{1,0:T(8,128)(2,1)} %x.1, bf16[512,1024]{1,0:T(8,128)(2,1)} %z.1, bf16[512,128]{1,0:T(8,128)(2,1)} %bm.1, ...), custom_call_target="tpu_custom_call" | custom-call | tf_op jit(solution)/shard_map/pallas_call | solution.py:778
  137.1 4.1 %shard_map.164 = (bf16[512,1024]{1,0:T(8,128)(2,1)}, bf16[512,1024]{1,0:T(8,128)(2,1)}, bf16[512,128]{1,0:T(8,128)(2,1)}, bf16[512,128]{1,0:T(8,128)(2,1)}, f32[16,512]{1,0:T(8,128)}, /*index=5*/f32[128,1024]{1,0:T(8,128)}) custom-call(bf16[512,1024]{1,0:T(8,128)(2,1)} %get-tuple-element.12.refs_0_, bf16[512,1024]{1,0:T(8,128)(2,1)} %get-tuple-element.13.refs_1_, ...), custom_call_target="tpu_custom_call" | custom-call | tf_op jit(solution)/shard_map/pallas_call | solution.py:788
Async XLA Ops:
  0.6 0.7 copy-start
